TPU v7x, 256 devices: a whole 4x4x8 slice. The times are simulated.
256 devices in a mesh: grp: 4 (over x), dev: 64 (over y, z, core).
Axes of the slice: x: 4, y: 4, z: 8, core: 2. Of those that a mesh axis runs over, the one named last changes fastest.
Arguments:
- positions: float32 [3, 65536], P(None, ('grp', 'dev')), may hold values from -1 to 1
- velocities: float32 [3, 65536], P(None, ('grp', 'dev')), may hold values from -4 to 4
- accel_old: float32 [3, 65536], P(None, ('grp', 'dev')), may hold values from -6 to 6
- jerk_old: float32 [3, 65536], P(None, ('grp', 'dev')), may hold values from -6 to 6
- masses: float32 [65536], P(('grp', 'dev')), may hold values from 3.0517579e-06 to 7.6293945e-05
- levels: int32 [65536], P(('grp', 'dev')), may hold values from 0 to 3
- live_count: int32 [256], P(('grp', 'dev')), may hold values from 128 to 256, as said below
- active_slot: int32 [32768], P(('grp', 'dev')), may hold values from 0 to 255, as said below
Outputs:
- pos_vel: float32 [6, 32768], P(None, ('grp', 'dev'))
- acc_jerk: float32 [6, 32768], P(None, ('grp', 'dev'))
- potential: float32 [32768], P(('grp', 'dev'))
Inputs may be any that keep to these rules, and one draw needn't show every extreme that they name: `live_count`: every entry is at least 128; some device is full with 256 and some has exactly 128; the counts are uneven across devices. `active_slot`: within each device's aligned block of 128 entries the slots are distinct and below that device's live_count.
All inputs are finite; a program needn't handle non-finite values.
Results may differ from a plain program's by a relative error of at most 0.00029.
Values sent between devices are 32-bit elements; how exact they have to be, the bound alone decides.
No kernel may reach another device: no remote copies, remote signals or barrier semaphores. Data moves between devices by JAX's collectives and lax.ppermute only.
A program may use at most 64 MiB of HBM per device.

v0:
```python
import jax
import jax.numpy as jnp
from jax import lax
from jax.sharding import PartitionSpec as P

tau_base = 0.5
soften_sq = 0.0001


def pair_terms(active_state, src_pos, src_vel, src_mass):
    delta_pos = src_pos[:, None, :] - active_state[0:3, :, None]
    delta_vel = src_vel[:, None, :] - active_state[3:6, :, None]
    dist_sq = jnp.sum(delta_pos * delta_pos, axis=0) + soften_sq
    weight = src_mass[None, :] / jnp.sqrt(dist_sq)
    cubed = weight / dist_sq
    radial = 3.0 * jnp.sum(delta_pos * delta_vel, axis=0) / dist_sq
    accel = jnp.sum(cubed[None] * delta_pos, axis=2)
    jerk_new = jnp.sum(cubed[None] * (delta_vel - radial[None] * delta_pos), axis=2)
    pot_sum = -jnp.sum(weight, axis=1)
    return jnp.concatenate([accel, jerk_new, pot_sum[None]], axis=0)


def correct(state, summed):
    pos_now = state[0:3]
    vel_now = state[3:6]
    acc_start = state[6:9]
    jerk_start = state[9:12]
    step_size = state[12:13]
    acc_end = summed[0:3]
    jerk_end = summed[3:6]
    differ = acc_start - acc_end
    fourth = -6.0 * differ - step_size * (4.0 * jerk_start + 2.0 * jerk_end)
    fifth = 12.0 * differ + 6.0 * step_size * (jerk_start + jerk_end)
    new_pos = (
        pos_now + step_size * step_size / 24.0 * fourth + step_size * step_size / 120.0 * fifth
    )
    new_vel = vel_now + step_size / 6.0 * fourth + step_size / 24.0 * fifth
    return (jnp.concatenate([new_pos, new_vel], axis=0), summed[0:6], summed[6])


def sweep_sources(active_state, pos_pred, vel_pred, live_mass):
    n_active = active_state.shape[1]
    block_size = min(512, n_active)
    blocks = active_state.reshape(6, n_active // block_size, block_size).transpose(1, 0, 2)

    def one_block(block):
        return pair_terms(block, pos_pred, vel_pred, live_mass)

    partial_value = lax.map(one_block, blocks)
    return partial_value.transpose(1, 0, 2).reshape(7, n_active)


def shards(positions, velocities, accel_old, jerk_old, masses, levels, live_count, active_slot):
    elapsed = tau_base * jnp.exp2(-levels.astype(jnp.float32))
    pos_pred = positions + elapsed * (
        velocities + elapsed * (accel_old / 2.0 + elapsed * jerk_old / 6.0)
    )
    vel_pred = velocities + elapsed * (accel_old + elapsed * jerk_old / 2.0)
    slots = jnp.arange(positions.shape[1], dtype=jnp.int32)
    live_mass = jnp.where(slots < live_count[0], masses, jnp.float32(0.0))
    owned = jnp.concatenate(
        [
            pos_pred[:, active_slot],
            vel_pred[:, active_slot],
            accel_old[:, active_slot],
            jerk_old[:, active_slot],
            elapsed[active_slot][None],
        ],
        axis=0,
    )
    active = lax.all_gather(owned[0:6], ("grp", "dev"), axis=1, tiled=True)
    partial_value = sweep_sources(active, pos_pred, vel_pred, live_mass)
    summed = lax.psum_scatter(partial_value, ("grp", "dev"), scatter_dimension=1, tiled=True)
    return correct(owned, summed)


def solution(mesh):
    return jax.shard_map(
        shards,
        mesh=mesh,
        in_specs=(
            P(None, ("grp", "dev")),
            P(None, ("grp", "dev")),
            P(None, ("grp", "dev")),
            P(None, ("grp", "dev")),
            P(("grp", "dev")),
            P(("grp", "dev")),
            P(("grp", "dev")),
            P(("grp", "dev")),
        ),
        out_specs=(P(None, ("grp", "dev")), P(None, ("grp", "dev")), P(("grp", "dev"))),
        check_vma=False,
    )
```

profile of v0, /device:TPU:1, one launch (start us, length us, event | category | flops | bytes accessed | tf_op | source)
XLA Modules:
  0.0 1475.5 jit_solution(7230137608994621387)
XLA Ops:
  11.1 67.8 %all_gather.3 = f32[6,32768]{1,0:T(8,128)S(1)} all-gather(f32[6,128]{1,0:T(8,128)S(1)} %pad_maximum_fusion), channel_id=1, replica_groups=mesh['grp'=4,'dev'=64] {'grp','dev'}, dimensions={1}, use_global_device_ids=true | all-gather | bytes 789504 | tf_op jit(solution)/shard_map/all_gather | solution.py:71
  79.5 109.0 %while.10 = (s32[]{:T(128)}, f32[64,7,512]{2,1,0:T(8,128)S(1)}, f32[256]{0:T(256)S(1)}, f32[3,256]{1,0:T(4,128)S(1)}, f32[64,6,512]{2,1,0:T(8,128)S(1)}, /*index...) while((s32[]{:T(128)}, f32[64,7,512]{2,1,0:T(8,128)S(1)}, f32[256]{0:T(256)S(1)}, f32[3,256]{1,0:T(4,128)S(1)}, ...), condition=%wide.region_6.7_spmd, body=%wide.region_0.6_spmd.sunk | while | flops 6033411 | bytes 4310133 | solution.py:49
  80.3 0.9 fusion.21
  82.0 0.9 fusion.21
  83.7 0.9 fusion.21
  85.4 0.9 fusion.21
  87.1 0.9 fusion.21
  88.8 0.9 fusion.21
  90.5 0.9 fusion.21
  92.2 0.9 fusion.21
  93.9 0.9 fusion.21
  95.6 0.9 fusion.21
  97.3 0.9 fusion.21
  99.0 0.9 fusion.21
  100.7 0.9 fusion.21
  102.4 0.9 fusion.21
  104.1 0.9 fusion.21
  105.8 0.9 fusion.21
  107.5 0.9 fusion.21
  109.2 0.9 fusion.21
  110.9 0.9 fusion.21
  112.6 0.9 fusion.21
  114.4 0.9 fusion.21
  116.1 0.9 fusion.21
  117.8 0.9 fusion.21
  119.5 0.9 fusion.21
  121.2 0.9 fusion.21
  122.9 0.9 fusion.21
  124.6 0.9 fusion.21
  126.3 0.9 fusion.21
  128.0 0.9 fusion.21
  129.7 0.9 fusion.21
  131.4 0.9 fusion.21
  133.1 0.9 fusion.21
  134.8 0.9 fusion.21
  136.5 0.9 fusion.21
  138.2 0.9 fusion.21
  139.9 0.9 fusion.21
  141.6 0.9 fusion.21
  143.3 0.9 fusion.21
  145.0 0.9 fusion.21
  150.1 0.9 fusion.21
  151.8 0.9 fusion.21
  153.5 0.9 fusion.21
  155.2 0.9 fusion.21
  156.9 0.9 fusion.21
  158.6 0.9 fusion.21
  160.3 0.9 fusion.21
  162.0 0.9 fusion.21
  167.2 0.9 fusion.21
  168.9 0.9 fusion.21
  170.6 0.9 fusion.21
  172.3 0.9 fusion.21
  174.0 0.9 fusion.21
  175.7 0.9 fusion.21
  177.4 0.9 fusion.21
  182.5 0.9 fusion.21
  184.2 0.9 fusion.21
  185.9 0.9 fusion.21
  187.6 0.9 fusion.21
  188.6 1.0 copy-done
  189.6 1.3 gather_fusion.1
  192.6 1273.5 %reduce-scatter.2.cloned.1.call-done = f32[7,128]{1,0:T(8,128)} async-done(((f32[7,32768]{1,0:T(8,128)}), f32[7,128]{1,0:T(8,128)}) %reduce-scatter.2.cloned.1.call-update) | async-done | bytes 3600 | tf_op jit(solution)/shard_map/reduce_scatter | solution.py:73
  1467.4 1.2 slice_bitcast_fusion
  (358 shorter events, 59.4 us)
Async XLA Ops:
  7.2 72.4 %copy-start.3 = (f32[256]{0:T(256)S(1)}, f32[256]{0:T(256)}, u32[]{:S(2)}) copy-start(f32[256]{0:T(256)} %param.14) | copy-start | bytes 3076
  7.2 1458.9 %reduce-scatter.2.cloned.1.call-start = ((), (), s32[]{:S(2)}) async-start(), calls=%async_computation.1 | async-start | bytes 1052672 | tf_op jit(solution)/shard_map/reduce_scatter | solution.py:73
  188.6 1.0 copy-start
  188.6 2.3 copy-start.1
  188.6 2.4 copy-start.2
Sparse Core Ops, SparseCore 0:
  189.7 1276.3 reduce-scatter.1
where the time goes:
time: 1480 us
  waiting for transfers between devices  1270 us (86%)
  other arithmetic  109 us (7%)
  blocking collectives  67.8 us (5%)
  between operations  14.8 us (1%)
    reduce_scatter x1, waiting for transfers between devices, shards(): lax.psum_scatter(partial_value, ('grp', 'dev'), scatter_dimension=1, tile...  1270 us
    all_gather x1, blocking collectives, shards(): active = lax.all_gather(owned[0:6], ('grp', 'dev'), axis=1, tiled=True)  67.8 us
    reduce_sum x64, other arithmetic, pair_terms(): accel = jnp.sum(cubed[None] * delta_pos, axis=2)  59.3 us
    reduce_sum x64, other arithmetic, pair_terms(): radial = 3.0 * jnp.sum(delta_pos * delta_vel, axis=0) / dist_sq  30.3 us
  transfers between devices with their start and end apart: 1, of which 1 were waited for; matrix products, arithmetic and copies ran while one was open for 0% of the time, Pallas kernels for 0%

commit v1 on v0

v1 whole, which is shorter than its diff:
```python
import functools
import jax
import jax.numpy as jnp
from jax import lax
from jax.experimental import pallas as pl
from jax.experimental.pallas import tpu as pltpu
from jax.sharding import Mesh, PartitionSpec as P

soften_sq = 0.0001
BF = jnp.bfloat16
F32 = jnp.float32


def round_bf(x):
    return x.astype(BF).astype(F32)


def pieces3(x):
    a = round_bf(x)
    r = x - a
    b = round_bf(r)
    return a, b, round_bf(r - b)


def row_ids(shape):
    return lax.broadcasted_iota(jnp.int32, shape, 0)


def grid_split(x):
    row = row_ids(x.shape)
    x = jnp.where(row < 6, x, 0.0)
    up = jnp.where(row < 3, 64.0, 32.0)
    down = jnp.where(row < 3, 1.0 / 64.0, 1.0 / 32.0)
    coarse = jnp.round(x * up) * down
    rest = x - coarse
    p1 = round_bf(rest)
    p2 = round_bf(rest - p1)
    return coarse, p1, p2


def stack_scalar(first, second, swapped):
    n = first.shape[1]
    one = jnp.ones((1, n), F32)
    zero = jnp.zeros((2, n), F32)
    a = pieces3(first)
    if swapped:
        return jnp.concatenate([one, one, one, *a, zero], axis=0)
    return jnp.concatenate([*a, one, one, one, zero], axis=0)


def scalars(coarse, p1, p2):
    fine = p1 + p2
    h, l = coarse[0:3], fine[0:3]
    vh, vl = coarse[3:6], fine[3:6]
    norm_exact = jnp.sum(h * h, axis=0, keepdims=True)
    norm_rest = jnp.sum(2.0 * h * l + l * l, axis=0, keepdims=True)
    dot_exact = jnp.sum(h * vh, axis=0, keepdims=True)
    dot_rest = jnp.sum(h * vl + l * vh + l * vl, axis=0, keepdims=True)
    return norm_exact, norm_rest, dot_exact, dot_rest


def source_features(x):
    c, p1, p2 = grid_split(x)
    ne, nr, de, dr = scalars(c, p1, p2)
    n = x.shape[1]
    s = [stack_scalar(v, None, False) for v in (ne, de, nr, dr)]
    zero = jnp.zeros((8, n), F32)
    return jnp.concatenate([s[0], s[1], c, p1, p2, c, c, p1, p2, p1, s[2], s[3], zero, zero, zero, zero], axis=0)


def active_features(x):
    c, p1, p2 = grid_split(x)
    ne, nr, de, dr = scalars(c, p1, p2)
    n = x.shape[1]
    row = row_ids(x.shape)

    def norm_side(t):
        return jnp.where(row < 3, -2.0 * t, 0.0)

    def dot_side(t):
        return jnp.concatenate([-t[3:6], -t[0:3], t[6:8]], axis=0)

    zero = jnp.zeros((8, n), F32)

    def build(side, exact, rest, is_norm):
        se = stack_scalar(exact, None, True)
        sr = stack_scalar(rest, None, True)
        first = [se, zero] if is_norm else [zero, se]
        last = [sr, zero] if is_norm else [zero, sr]
        h, a, b = side(c), side(p1), side(p2)
        return jnp.concatenate([*first, h, h, h, a, b, a, a, b, *last, zero, zero, zero, zero], axis=0)

    return build(norm_side, ne, nr + soften_sq, True), build(dot_side, de, dr, False)


def reduce_rows(x):
    row = row_ids(x.shape)
    mass = x[6:7]
    y = jnp.where(row < 6, x, jnp.where(row == 6, 1.0, 0.0)) * mass
    a, b, c = pieces3(y)
    return jnp.concatenate([a, b, c, jnp.zeros_like(a)], axis=0)


def split_hi_lo(t):
    hi = t.astype(BF)
    return hi, (t - hi.astype(F32)).astype(BF)


def pair_kernel(n_src, n_act, act_ref, src_ref, out_ref, dense, feat_j, feat_q, feat_d, red_ref, acc_u, acc_p, acc_w):
    tile = 256
    total_act = n_act * 128
    width = n_src * 256 + 512
    for t in range(width // 128):
        dense[:, t * 128:(t + 1) * 128] = jnp.zeros((8, 128), F32)
    lane = lax.broadcasted_iota(jnp.int32, (8, 128), 1)
    counts = [jnp.max(src_ref[b, 7:8, 0:128]).astype(jnp.int32) for b in range(n_src)]
    offset = jnp.int32(0)
    for b in range(n_src):
        shift = lax.rem(offset, 128)
        start = pl.multiple_of(offset - shift, 128)
        left = pltpu.roll(src_ref[b, :, 0:128], shift, 1)
        right = pltpu.roll(src_ref[b, :, 128:256], shift, 1)
        before = lane < shift
        dense[:, pl.ds(start, 128)] = jnp.where(before, dense[:, pl.ds(start, 128)], left)
        dense[:, pl.ds(start + 128, 128)] = jnp.where(before, left, right)
        dense[:, pl.ds(start + 256, 128)] = jnp.where(before, right, 0.0)
        offset = offset + counts[b]
    n_blocks = (offset + (tile - 1)) // tile
    for k in range(n_act):
        fq, fd = active_features(act_ref[k])
        feat_q[:, k * 128:(k + 1) * 128] = fq.astype(BF)
        feat_d[:, k * 128:(k + 1) * 128] = fd.astype(BF)
    acc_u[...] = jnp.zeros_like(acc_u)
    acc_p[...] = jnp.zeros_like(acc_p)
    acc_w[...] = jnp.zeros_like(acc_w)

    def block(b, _):
        x = dense[:, pl.ds(pl.multiple_of(b * tile, tile), tile)]
        feat_j[...] = source_features(x).T.astype(BF)
        red_ref[...] = reduce_rows(x).astype(BF)

        def tiles(i, _):
            lanes = pl.ds(pl.multiple_of(i * tile, tile), tile)
            fj = feat_j[...]
            q = jnp.dot(fj, feat_q[:, lanes], preferred_element_type=F32)
            d = jnp.dot(fj, feat_d[:, lanes], preferred_element_type=F32)
            s = lax.rsqrt(q)
            s2 = s * s
            u = s * s2
            p = (u * s2) * d
            u_hi, u_lo = split_hi_lo(u)
            p_hi, p_lo = split_hi_lo(p)
            w = s.astype(BF)
            rows = red_ref[...]
            two = rows[0:16]
            def mm(a, b):
                return jnp.dot(a, b, preferred_element_type=F32)
            ru = mm(rows, u_hi)
            rp = mm(rows, p_hi)
            rul = mm(two, u_lo)
            rpl = mm(two, p_lo)
            rw = mm(two, w)
            acc_u[:, lanes] += (ru[0:8] + ru[8:16]) + (ru[16:24] + (rul[0:8] + rul[8:16]))
            acc_p[:, lanes] += (rp[0:8] + rp[8:16]) + (rp[16:24] + (rpl[0:8] + rpl[8:16]))
            acc_w[:, lanes] += rw[0:8] + rw[8:16]
            return 0

        lax.fori_loop(0, total_act // tile, tiles, 0)
        return 0

    lax.fori_loop(0, n_blocks, block, 0)
    for k in range(n_act):
        lanes = slice(k * 128, (k + 1) * 128)
        su = acc_u[:, lanes]
        sp = acc_p[:, lanes]
        sw = acc_w[:, lanes]
        st = act_ref[k]
        accel = su[0:3] - st[0:3] * su[6:7]
        jerk = su[3:6] - st[3:6] * su[6:7] - 3.0 * (sp[0:3] - st[0:3] * sp[6:7])
        out_ref[k] = jnp.concatenate([accel, jerk, -sw[6:7], jnp.zeros((1, 128), F32)], axis=0)


def pair_sums(actives, sources):
    n_act, n_src = actives.shape[0], sources.shape[0]
    total = n_act * 128
    return pl.pallas_call(
        functools.partial(pair_kernel, n_src, n_act),
        out_shape=jax.ShapeDtypeStruct((n_act, 8, 128), F32),
        in_specs=[pl.BlockSpec(memory_space=pltpu.VMEM)] * 2,
        out_specs=pl.BlockSpec(memory_space=pltpu.VMEM),
        scratch_shapes=[
            pltpu.VMEM((8, n_src * 256 + 512), F32),
            pltpu.VMEM((256, 128), BF),
            pltpu.VMEM((128, total), BF),
            pltpu.VMEM((128, total), BF),
            pltpu.VMEM((32, 256), BF),
            pltpu.VMEM((8, total), F32),
            pltpu.VMEM((8, total), F32),
            pltpu.VMEM((8, total), F32),
        ],
        name="pair_sums",
        cost_estimate=pl.CostEstimate(flops=400_000_000, bytes_accessed=400_000, transcendentals=8_000_000),
    )(actives, sources)


def pick(table, slot):
    rows = []
    for k in range(table.shape[0] // 8):
        part = table[8 * k:8 * k + 8]
        low = jnp.broadcast_to(lax.rem(slot, 128), (8, 128))
        left = jnp.take_along_axis(part[:, 0:128], low, axis=1)
        right = jnp.take_along_axis(part[:, 128:256], low, axis=1)
        rows.append(jnp.where(slot < 128, left, right))
    return jnp.concatenate(rows, axis=0)


def predict_kernel(pos_ref, vel_ref, acc_ref, jerk_ref, mass_ref, level_ref, live_ref, slot_ref, src_ref, own_ref, act_ref):
    level = level_ref[...]
    half = jnp.where((level & 1) == 1, 0.5, 1.0)
    h = 0.5 * half * jnp.where((level & 2) == 2, 0.25, 1.0)
    acc, jerk, vel = acc_ref[...], jerk_ref[...], vel_ref[...]
    pos_pred = pos_ref[...] + h * (vel + h * (acc / 2.0 + h * jerk / 6.0))
    vel_pred = vel + h * (acc + h * jerk / 2.0)
    slots = lax.broadcasted_iota(jnp.int32, (1, 256), 1)
    count = live_ref[0]
    mass = jnp.where(slots < count, mass_ref[...], 0.0)
    counts = jnp.full((1, 256), count, jnp.int32).astype(F32)
    src = jnp.concatenate([pos_pred, vel_pred, mass, counts], axis=0)
    for k in range(src_ref.shape[0]):
        src_ref[k] = src
    rest = jnp.concatenate([acc, jerk, h, h], axis=0)
    own = pick(jnp.concatenate([src, rest], axis=0), slot_ref[...])
    own_ref[...] = own
    for k in range(act_ref.shape[0]):
        act_ref[k] = own[0:8]


def correct_kernel(own_ref, part_ref, state_ref, deriv_ref, pot_ref):
    summed = part_ref[0]
    for k in range(1, part_ref.shape[0]):
        summed = summed + part_ref[k]
    own = own_ref[...]
    pos_now, vel_now = own[0:3], own[3:6]
    acc_start, jerk_start, step = own[8:11], own[11:14], own[14:15]
    acc_end, jerk_end = summed[0:3], summed[3:6]
    differ = acc_start - acc_end
    fourth = -6.0 * differ - step * (4.0 * jerk_start + 2.0 * jerk_end)
    fifth = 12.0 * differ + 6.0 * step * (jerk_start + jerk_end)
    new_pos = pos_now + step * step / 24.0 * fourth + step * step / 120.0 * fifth
    new_vel = vel_now + step / 6.0 * fourth + step / 24.0 * fifth
    state_ref[...] = jnp.concatenate([new_pos, new_vel], axis=0)
    deriv_ref[...] = summed[0:6]
    pot_ref[...] = summed[6:7]


VM = pl.BlockSpec(memory_space=pltpu.VMEM)
SM = pl.BlockSpec(memory_space=pltpu.SMEM)
SRC_AXES = ("y", "z")
ACT_AXES = ("x", "c")


def shards(positions, velocities, accel_old, jerk_old, masses, levels, live_count, active_slot):
    n_src, n_act = 32, 8
    src, own, act = pl.pallas_call(
        predict_kernel,
        out_shape=(
            jax.ShapeDtypeStruct((n_src, 8, 256), F32),
            jax.ShapeDtypeStruct((16, 128), F32),
            jax.ShapeDtypeStruct((n_act, 8, 128), F32),
        ),
        in_specs=[VM, VM, VM, VM, VM, VM, SM, VM],
        out_specs=(VM, VM, VM),
        name="predict",
    )(positions, velocities, accel_old, jerk_old, masses[None], levels[None], live_count, active_slot[None])
    actives = lax.all_to_all(act, ACT_AXES, 0, 0)
    sources = lax.all_to_all(src, SRC_AXES, 0, 0)
    partial_sums = pair_sums(actives, sources)
    parts = lax.all_to_all(partial_sums, ACT_AXES, 0, 0)
    state, deriv, pot = pl.pallas_call(
        correct_kernel,
        out_shape=(
            jax.ShapeDtypeStruct((6, 128), F32),
            jax.ShapeDtypeStruct((6, 128), F32),
            jax.ShapeDtypeStruct((1, 128), F32),
        ),
        in_specs=[VM, VM],
        out_specs=(VM, VM, VM),
        name="correct",
    )(own, parts)
    return state, deriv, pot[0]


def solution(mesh):
    fine = Mesh(mesh.devices.reshape(4, 4, 8, 2), ("x", "y", "z", "c"))
    every = ("x", "y", "z", "c")
    rows, flat = P(None, every), P(every)
    return jax.shard_map(
        shards,
        mesh=fine,
        in_specs=(rows, rows, rows, rows, flat, flat, flat, flat),
        out_specs=(rows, rows, flat),
        check_vma=False,
    )
```

time: 1480 us -> 90.9 us (0.06)
  waiting for transfers between devices: 1270 us -> 0 us
  other arithmetic: 109 us -> 0 us
  Pallas kernels: 0 us -> 45.2 us
  blocking collectives: 67.8 us -> 43.9 us
    reduce_scatter x1 -> x0, waiting for transfers between devices: 1270 us -> none  [shards(): lax.psum_scatter(partial_value, ('grp', 'dev'), scatter_dimension=1, tile...]
    reduce_sum x128 -> x0, other arithmetic: 89.6 us -> none  [the longest x64 59.3 us: pair_terms(): accel = jnp.sum(cubed[None] * delta_pos, axis=2)]
    all_gather x1 -> x0, blocking collectives: 67.8 us -> none  [shards(): active = lax.all_gather(owned[0:6], ('grp', 'dev'), axis=1, tiled=True)]
    pallas_call x0 -> x3, Pallas kernels: none -> 45.2 us  [the longest x1 42.3 us: pair_sums(): pl.pallas_call(functools.partial(pair_kernel, n_src, n_act), out_shape=ja...]
    all_to_all x0 -> x3, blocking collectives: none -> 43.9 us  [the longest x1 19.8 us: shards(): sources = lax.all_to_all(src, SRC_AXES, 0, 0)]
  transfers between devices with their start and end apart: 1 -> 0, of which waited for: 1 -> 0; matrix products, arithmetic and copies ran while one was open for 0% -> 0% of each run, Pallas kernels for 0% -> 0%
where the time goes in v1:
time: 90.9 us; the launch traced here: 90.5 us
  Pallas kernels  45.2 us (50%)
  blocking collectives  43.9 us (48%)
  between operations  1.28 us (1%)
    pallas_call x1, Pallas kernels, pair_sums(): pl.pallas_call(functools.partial(pair_kernel, n_src, n_act), out_shape=ja...  42.3 us
    all_to_all x1, blocking collectives, shards(): sources = lax.all_to_all(src, SRC_AXES, 0, 0)  19.8 us
    all_to_all x1, blocking collectives, shards(): parts = lax.all_to_all(partial_sums, ACT_AXES, 0, 0)  12.3 us
    all_to_all x1, blocking collectives, shards(): actives = lax.all_to_all(act, ACT_AXES, 0, 0)  11.8 us

profile of v1, /device:TPU:1, one launch (start us, length us, event | category | flops | bytes accessed | tf_op | source)
XLA Modules:
  0.0 90.5 jit_solution(5519734582728589535)
XLA Ops:
  1.3 1.5 %predict.1 = (f32[32,8,256]{2,1,0:T(8,128)}, f32[16,128]{1,0:T(8,128)}, f32[8,8,128]{2,1,0:T(8,128)}) custom-call(f32[3,256]{1,0:T(4,128)} %pos_ref.1, f32[3,256]{1,0:T(4,128)} %vel_ref.1, f32[3,256]{1,0:T(4,128)} %acc_ref.1, f32[3,256]{1,0:T(4,128)} %jerk_ref.1, f32[1,256]{1,0:T(1,128)} %bitcast.4, s32[1,256]{1,0:T(1,128)} %bitcast.5, s32[1]{0:T(128)S(6)} %copy.11.live_ref, ...), custom_call_target="tpu_custom_call" | custom-call | tf_op jit(solution)/shard_map/predict/pallas_call | solution.py:264
  2.8 11.8 %all_to_all.15.act_ref = f32[8,8,128]{2,1,0:T(8,128)} all-to-all(f32[8,8,128]{2,1,0:T(8,128)} %get-tuple-element.10), channel_id=1, replica_groups=mesh['x'=4,'y'=4,'z'=8,'c'=2] {'x','c'}, dimensions={0} | all-to-all | bytes 65536 | tf_op jit(solution)/shard_map/all_to_all | solution.py:275
  14.6 19.8 %all_to_all.16.src_ref = f32[32,8,256]{2,1,0:T(8,128)} all-to-all(f32[32,8,256]{2,1,0:T(8,128)} %get-tuple-element.11), channel_id=1, replica_groups=mesh['x'=4,'y'=4,'z'=8,'c'=2] {'y','z'}, dimensions={0} | all-to-all | bytes 524288 | tf_op jit(solution)/shard_map/all_to_all | solution.py:276
  34.4 42.3 %pair_sums.1 = f32[8,8,128]{2,1,0:T(8,128)} custom-call(f32[8,8,128]{2,1,0:T(8,128)} %all_to_all.15.act_ref, f32[32,8,256]{2,1,0:T(8,128)} %all_to_all.16.src_ref), custom_call_target="tpu_custom_call" | custom-call | flops 400000000 | bytes 400000 | tf_op jit(solution)/shard_map/pair_sums/pallas_call | solution.py:186
  76.7 12.3 %all_to_all.17.part_ref = f32[8,8,128]{2,1,0:T(8,128)} all-to-all(f32[8,8,128]{2,1,0:T(8,128)} %pair_sums.1), channel_id=1, replica_groups=mesh['x'=4,'y'=4,'z'=8,'c'=2] {'x','c'}, dimensions={0} | all-to-all | bytes 65536 | tf_op jit(solution)/shard_map/all_to_all | solution.py:278
  89.1 1.4 %correct.1 = (f32[6,128]{1,0:T(8,128)}, f32[6,128]{1,0:T(8,128)}, f32[1,128]{1,0:T(1,128)}) custom-call(f32[16,128]{1,0:T(8,128)} %get-tuple-element.9.own_ref, f32[8,8,128]{2,1,0:T(8,128)} %all_to_all.17.part_ref), custom_call_target="tpu_custom_call" | custom-call | tf_op jit(solution)/shard_map/correct/pallas_call | solution.py:279

commit v2 on v1

--- a/solution.py
+++ b/solution.py
@@ -106,9 +106,11 @@
     return hi, (t - hi.astype(F32)).astype(BF)
 
 
-def pair_kernel(n_src, n_act, act_ref, src_ref, out_ref, dense, feat_j, feat_q, feat_d, red_ref, acc_u, acc_p, acc_w):
+def pair_kernel(n_src, n_act, act_ref, src_ref, out_ref, dense, feat_j, feat_q, feat_d, red_ref, acc_u, acc_p, acc_w, *bufs):
     tile = 256
-    total_act = n_act * 128
+    n_tiles = n_act * 128 // tile
+    q_bufs, d_bufs = bufs[0:2], bufs[2:4]
+    v_bufs = bufs[4:6]
     width = n_src * 256 + 512
     for t in range(width // 128):
         dense[:, t * 128:(t + 1) * 128] = jnp.zeros((8, 128), F32)
@@ -125,50 +127,76 @@
         dense[:, pl.ds(start + 128, 128)] = jnp.where(before, left, right)
         dense[:, pl.ds(start + 256, 128)] = jnp.where(before, right, 0.0)
         offset = offset + counts[b]
-    n_blocks = (offset + (tile - 1)) // tile
+    n_pairs = (offset + (2 * tile - 1)) // (2 * tile)
     for k in range(n_act):
         fq, fd = active_features(act_ref[k])
-        feat_q[:, k * 128:(k + 1) * 128] = fq.astype(BF)
-        feat_d[:, k * 128:(k + 1) * 128] = fd.astype(BF)
+        feat_q[k] = fq.astype(BF)
+        feat_d[k] = fd.astype(BF)
     acc_u[...] = jnp.zeros_like(acc_u)
     acc_p[...] = jnp.zeros_like(acc_p)
     acc_w[...] = jnp.zeros_like(acc_w)
-
-    def block(b, _):
-        x = dense[:, pl.ds(pl.multiple_of(b * tile, tile), tile)]
-        feat_j[...] = source_features(x).T.astype(BF)
-        red_ref[...] = reduce_rows(x).astype(BF)
-
-        def tiles(i, _):
-            lanes = pl.ds(pl.multiple_of(i * tile, tile), tile)
-            fj = feat_j[...]
-            q = jnp.dot(fj, feat_q[:, lanes], preferred_element_type=F32)
-            d = jnp.dot(fj, feat_d[:, lanes], preferred_element_type=F32)
+    red_ref[...] = jnp.zeros_like(red_ref)
+    v_bufs[1][...] = jnp.zeros_like(v_bufs[1])
+
+    def sources(b):
+        return dense[:, pl.ds(pl.multiple_of(b * tile, tile), tile)]
+
+    def wide(ref, *at):
+        return jnp.concatenate([ref[(*at, 0)], ref[(*at, 1)]], axis=1)
+
+    def generate(i):
+        fj = feat_j[...]
+        fq = jnp.concatenate([feat_q[2 * i], feat_q[2 * i + 1]], axis=1)
+        fd = jnp.concatenate([feat_d[2 * i], feat_d[2 * i + 1]], axis=1)
+        q_bufs[i % 2][...] = jnp.dot(fj, fq, preferred_element_type=F32)
+        d_bufs[i % 2][...] = jnp.dot(fj, fd, preferred_element_type=F32)
+
+    def combine(i):
+        v = v_bufs[i % 2]
+        for half in range(2):
+            lanes = slice(half * 128, half * 128 + 128)
+            q = q_bufs[i % 2][:, lanes]
+            d = d_bufs[i % 2][:, lanes]
             s = lax.rsqrt(q)
             s2 = s * s
             u = s * s2
             p = (u * s2) * d
-            u_hi, u_lo = split_hi_lo(u)
-            p_hi, p_lo = split_hi_lo(p)
-            w = s.astype(BF)
-            rows = red_ref[...]
-            two = rows[0:16]
-            def mm(a, b):
-                return jnp.dot(a, b, preferred_element_type=F32)
-            ru = mm(rows, u_hi)
-            rp = mm(rows, p_hi)
-            rul = mm(two, u_lo)
-            rpl = mm(two, p_lo)
-            rw = mm(two, w)
-            acc_u[:, lanes] += (ru[0:8] + ru[8:16]) + (ru[16:24] + (rul[0:8] + rul[8:16]))
-            acc_p[:, lanes] += (rp[0:8] + rp[8:16]) + (rp[16:24] + (rpl[0:8] + rpl[8:16]))
-            acc_w[:, lanes] += rw[0:8] + rw[8:16]
-            return 0
-
-        lax.fori_loop(0, total_act // tile, tiles, 0)
+            v[0, half], v[1, half] = split_hi_lo(u)
+            v[2, half], v[3, half] = split_hi_lo(p)
+            v[4, half] = s.astype(BF)
+
+    def reduce(i):
+        v = v_bufs[i % 2]
+        lanes = slice(i * tile, (i + 1) * tile)
+        rows = red_ref[...]
+        two = rows[0:16]
+
+        def mm(a, k):
+            return jnp.dot(a, wide(v, k), preferred_element_type=F32)
+
+        ru, rul, rp, rpl, rw = mm(rows, 0), mm(two, 1), mm(rows, 2), mm(two, 3), mm(two, 4)
+        acc_u[:, lanes] += (ru[0:8] + ru[8:16]) + (ru[16:24] + (rul[0:8] + rul[8:16]))
+        acc_p[:, lanes] += (rp[0:8] + rp[8:16]) + (rp[16:24] + (rpl[0:8] + rpl[8:16]))
+        acc_w[:, lanes] += rw[0:8] + rw[8:16]
+
+    feat_j[...] = source_features(sources(0)).T.astype(BF)
+    generate(0)
+
+    def pair(k, _):
+        for b in (2 * k, 2 * k + 1):
+            fresh = source_features(sources(b + 1)).T.astype(BF)
+            for i in range(n_tiles):
+                if i == n_tiles - 1:
+                    feat_j[...] = fresh
+                generate((i + 1) % n_tiles)
+                combine(i)
+                reduce((i - 1) % n_tiles)
+                if i == 0:
+                    red_ref[...] = reduce_rows(sources(b)).astype(BF)
         return 0
 
-    lax.fori_loop(0, n_blocks, block, 0)
+    lax.fori_loop(0, n_pairs, pair, 0)
+    reduce(n_tiles - 1)
     for k in range(n_act):
         lanes = slice(k * 128, (k + 1) * 128)
         su = acc_u[:, lanes]
@@ -191,12 +219,14 @@
         scratch_shapes=[
             pltpu.VMEM((8, n_src * 256 + 512), F32),
             pltpu.VMEM((256, 128), BF),
-            pltpu.VMEM((128, total), BF),
-            pltpu.VMEM((128, total), BF),
+            pltpu.VMEM((n_act, 128, 128), BF),
+            pltpu.VMEM((n_act, 128, 128), BF),
             pltpu.VMEM((32, 256), BF),
             pltpu.VMEM((8, total), F32),
             pltpu.VMEM((8, total), F32),
             pltpu.VMEM((8, total), F32),
+            *[pltpu.VMEM((256, 256), F32) for _ in range(4)],
+            *[pltpu.VMEM((5, 2, 256, 128), BF) for _ in range(2)],
         ],
         name="pair_sums",
         cost_estimate=pl.CostEstimate(flops=400_000_000, bytes_accessed=400_000, transcendentals=8_000_000),

time: 90.9 us -> 69.1 us (0.76)
  Pallas kernels: 45.2 us -> 24.1 us
  blocking collectives: 43.9 us -> 42.6 us
    pallas_call x1, Pallas kernels: 42.3 us -> 21.2 us  [pair_sums(): pl.pallas_call(functools.partial(pair_kernel, n_src, n_act), out_shape=ja...]
    all_to_all x1, blocking collectives: 12.3 us -> 11 us  [shards(): parts = lax.all_to_all(partial_sums, ACT_AXES, 0, 0)]
where the time goes in v2:
time: 69.1 us; the launch traced here: 68 us
  blocking collectives  42.6 us (62%)
  Pallas kernels  24.1 us (35%)
  between operations  1.28 us (2%)
    pallas_call x1, Pallas kernels, pair_sums(): pl.pallas_call(functools.partial(pair_kernel, n_src, n_act), out_shape=ja...  21.2 us
    all_to_all x1, blocking collectives, shards(): sources = lax.all_to_all(src, SRC_AXES, 0, 0)  19.8 us
    all_to_all x1, blocking collectives, shards(): actives = lax.all_to_all(act, ACT_AXES, 0, 0)  11.8 us
    all_to_all x1, blocking collectives, shards(): parts = lax.all_to_all(partial_sums, ACT_AXES, 0, 0)  11 us
    pallas_call x1, Pallas kernels, shards(): pl.pallas_call(predict_kernel, out_shape=(jax.ShapeDtypeStruct((n_src, 8,...  1.52 us
    pallas_call x1, Pallas kernels, shards(): pl.pallas_call(correct_kernel, out_shape=(jax.ShapeDtypeStruct((6, 128),...  1.39 us

profile of v2, /device:TPU:1, one launch (start us, length us, event | category | flops | bytes accessed | tf_op | source)
XLA Modules:
  0.0 68.0 jit_solution(7392781887736523185)
XLA Ops:
  1.3 1.5 %predict.1 = (f32[32,8,256]{2,1,0:T(8,128)}, f32[16,128]{1,0:T(8,128)}, f32[8,8,128]{2,1,0:T(8,128)}) custom-call(f32[3,256]{1,0:T(4,128)} %pos_ref.1, f32[3,256]{1,0:T(4,128)} %vel_ref.1, f32[3,256]{1,0:T(4,128)} %acc_ref.1, f32[3,256]{1,0:T(4,128)} %jerk_ref.1, f32[1,256]{1,0:T(1,128)} %bitcast.4, s32[1,256]{1,0:T(1,128)} %bitcast.5, s32[1]{0:T(128)S(6)} %copy.11.live_ref, ...), custom_call_target="tpu_custom_call" | custom-call | tf_op jit(solution)/shard_map/predict/pallas_call | solution.py:294
  2.8 11.8 %all_to_all.15.act_ref = f32[8,8,128]{2,1,0:T(8,128)} all-to-all(f32[8,8,128]{2,1,0:T(8,128)} %get-tuple-element.10), channel_id=1, replica_groups=mesh['x'=4,'y'=4,'z'=8,'c'=2] {'x','c'}, dimensions={0} | all-to-all | bytes 65536 | tf_op jit(solution)/shard_map/all_to_all | solution.py:305
  14.6 19.8 %all_to_all.16.src_ref = f32[32,8,256]{2,1,0:T(8,128)} all-to-all(f32[32,8,256]{2,1,0:T(8,128)} %get-tuple-element.11), channel_id=1, replica_groups=mesh['x'=4,'y'=4,'z'=8,'c'=2] {'y','z'}, dimensions={0} | all-to-all | bytes 524288 | tf_op jit(solution)/shard_map/all_to_all | solution.py:306
  34.4 21.2 %pair_sums.1 = f32[8,8,128]{2,1,0:T(8,128)} custom-call(f32[8,8,128]{2,1,0:T(8,128)} %all_to_all.15.act_ref, f32[32,8,256]{2,1,0:T(8,128)} %all_to_all.16.src_ref), custom_call_target="tpu_custom_call" | custom-call | flops 400000000 | bytes 400000 | tf_op jit(solution)/shard_map/pair_sums/pallas_call | solution.py:214
  55.6 11.0 %all_to_all.17.part_ref = f32[8,8,128]{2,1,0:T(8,128)} all-to-all(f32[8,8,128]{2,1,0:T(8,128)} %pair_sums.1), channel_id=1, replica_groups=mesh['x'=4,'y'=4,'z'=8,'c'=2] {'x','c'}, dimensions={0} | all-to-all | bytes 65536 | tf_op jit(solution)/shard_map/all_to_all | solution.py:308
  66.6 1.4 %correct.1 = (f32[6,128]{1,0:T(8,128)}, f32[6,128]{1,0:T(8,128)}, f32[1,128]{1,0:T(1,128)}) custom-call(f32[16,128]{1,0:T(8,128)} %get-tuple-element.9.own_ref, f32[8,8,128]{2,1,0:T(8,128)} %all_to_all.17.part_ref), custom_call_target="tpu_custom_call" | custom-call | tf_op jit(solution)/shard_map/correct/pallas_call | solution.py:309

commit v3 on v2

v3 whole, which is shorter than its diff:
```python
import functools
import jax
import jax.numpy as jnp
from jax import lax
from jax.experimental import pallas as pl
from jax.experimental.pallas import tpu as pltpu
from jax.sharding import Mesh, PartitionSpec as P

soften_sq = 0.0001
BF = jnp.bfloat16
F32 = jnp.float32


def round_bf(x):
    return x.astype(BF).astype(F32)


def pieces3(x):
    a = round_bf(x)
    r = x - a
    b = round_bf(r)
    return a, b, r - b


def row_ids(shape):
    return lax.broadcasted_iota(jnp.int32, shape, 0)


def grid_split(x):
    row = row_ids(x.shape)
    up = jnp.where(row < 3, 64.0, jnp.where(row < 6, 32.0, 0.0))
    down = jnp.where(row < 3, 1.0 / 64.0, 1.0 / 32.0)
    coarse = jnp.round(x * up) * down
    rest = jnp.where(row < 6, x - coarse, 0.0)
    p1 = round_bf(rest)
    p2 = round_bf(rest - p1)
    return coarse, p1, p2


def twice(t):
    return jnp.where(row_ids(t.shape) < 3, t, pltpu.roll(t, 3, 0))


def squares(coarse, p1, p2):
    fine = p1 + p2
    t, l = twice(coarse), twice(fine)
    return coarse * t, coarse * l + fine * (t + l)


def source_features(x):
    c, p1, p2 = grid_split(x)
    exact, rest = squares(c, p1, p2)
    e1 = round_bf(exact)
    r1, r2, r3 = pieces3(rest)
    one = jnp.ones_like(c)
    zero = jnp.zeros_like(c)
    parts = [e1, exact - e1, one, c, p1, p2, c, c, p1, p2, p1, r1, r2, r3, one, zero]
    return jnp.concatenate([jnp.concatenate(parts[k:k + 2], axis=0).astype(BF) for k in range(0, 16, 2)], axis=0).T


def active_features(x):
    c, p1, p2 = grid_split(x)
    exact, rest = squares(c, p1, p2)
    row = row_ids(x.shape)
    one = jnp.ones_like(c)

    def sums(t, first):
        return jnp.sum(t[first:first + 3], axis=0, keepdims=True)

    def stack(t):
        return jnp.concatenate([*pieces3(t), jnp.zeros((5, t.shape[1]), F32)], axis=0)

    def norm_side(t):
        return jnp.where(row < 3, -2.0 * t, 0.0)

    def dot_side(t):
        return jnp.concatenate([-t[3:6], -t[0:3], jnp.zeros_like(t[6:8])], axis=0)

    def build(side, first, soften):
        pick_rows = jnp.where((row >= first) & (row < first + 3), one, 0.0)
        h, a, b = side(c), side(p1), side(p2)
        same = [pick_rows] * 3
        parts = [*same[:2], stack(sums(exact, first)), h, h, h, a, b, a, a, b, *same, stack(sums(rest, first) + soften), 0.0 * one]
        return jnp.concatenate(parts, axis=0)

    return build(norm_side, 0, soften_sq), build(dot_side, 3, 0.0)


def reduce_rows(x):
    row = row_ids(x.shape)
    c, p1, p2 = grid_split(x)
    near = c + (p1 + p2)
    square = near * near
    norm = square + (pltpu.roll(square, 7, 0) + pltpu.roll(square, 6, 0))
    y = jnp.where(row < 6, near, jnp.where(row == 6, 1.0, pltpu.roll(norm, 7, 0))) * x[6:7]
    a, b, c = pieces3(y)
    return jnp.concatenate([a, b, c, jnp.zeros_like(a)], axis=0)


def split_hi_lo(t):
    hi = t.astype(BF)
    return hi, (t - hi.astype(F32)).astype(BF)


def pair_kernel(n_src, n_act, near_ref, far_ref, src_ref, out_ref, dense, feat_j, feat_q, feat_d, red_ref, acc_u, acc_p, *bufs):
    tile = 256
    n_tiles = n_act * 128 // tile
    me = 2 * lax.axis_index("x") + lax.axis_index("c")

    def active(k):
        return near_ref[k] if k < n_act // 2 else far_ref[k - n_act // 2]

    q_bufs, d_bufs, v_bufs = (bufs[k * n_tiles:(k + 1) * n_tiles] for k in range(3))
    width = n_src * 256 + 768
    for t in range(width // 128):
        dense[:, t * 128:(t + 1) * 128] = jnp.zeros((8, 128), F32)
    lane = lax.broadcasted_iota(jnp.int32, (8, 128), 1)
    counts = [jnp.max(src_ref[b, 7:8, 0:128]).astype(jnp.int32) for b in range(n_src)]
    offset = jnp.int32(0)
    for b in range(n_src):
        shift = lax.rem(offset, 128)
        start = pl.multiple_of(offset - shift, 128)
        left = pltpu.roll(src_ref[b, :, 0:128], shift, 1)
        right = pltpu.roll(src_ref[b, :, 128:256], shift, 1)
        before = lane < shift
        dense[:, pl.ds(start, 128)] = jnp.where(before, dense[:, pl.ds(start, 128)], left)
        dense[:, pl.ds(start + 128, 128)] = jnp.where(before, left, right)
        dense[:, pl.ds(start + 256, 128)] = jnp.where(before, right, 0.0)
        offset = offset + counts[b]
    n_blocks = (offset + (tile - 1)) // tile
    for k in range(n_act):
        fq, fd = active_features(active(k))
        feat_q[k] = fq.astype(BF)
        feat_d[k] = fd.astype(BF)
    acc_u[...] = jnp.zeros_like(acc_u)
    acc_p[...] = jnp.zeros_like(acc_p)

    def sources(b):
        return dense[:, pl.ds(pl.multiple_of(b * tile, tile), tile)]

    def wide(ref, *at):
        return jnp.concatenate([ref[(*at, 0)], ref[(*at, 1)]], axis=1)

    def generate(i):
        fj = feat_j[...]
        fq = jnp.concatenate([feat_q[2 * i], feat_q[2 * i + 1]], axis=1)
        fd = jnp.concatenate([feat_d[2 * i], feat_d[2 * i + 1]], axis=1)
        q_bufs[i][...] = jnp.dot(fj, fq, preferred_element_type=F32)
        d_bufs[i][...] = jnp.dot(fj, fd, preferred_element_type=F32)

    def combine(i):
        v = v_bufs[i]
        for half in range(2):
            lanes = slice(half * 128, half * 128 + 128)
            q = q_bufs[i][:, lanes]
            d = d_bufs[i][:, lanes]
            s = lax.rsqrt(q)
            s2 = s * s
            u = s * s2
            p = (u * s2) * d
            v[0, half], v[1, half] = split_hi_lo(u)
            v[2, half], v[3, half] = split_hi_lo(p)

    def reduce(i):
        v = v_bufs[i]
        lanes = slice(i * tile, (i + 1) * tile)
        rows = red_ref[...]
        two = rows[0:16]

        def mm(a, k):
            return jnp.dot(a, wide(v, k), preferred_element_type=F32)

        ru, rul, rp, rpl = mm(rows, 0), mm(two, 1), mm(rows, 2), mm(two, 3)
        acc_u[:, lanes] += (ru[0:8] + ru[8:16]) + (ru[16:24] + (rul[0:8] + rul[8:16]))
        acc_p[:, lanes] += (rp[0:8] + rp[8:16]) + (rp[16:24] + (rpl[0:8] + rpl[8:16]))

    feat_j[...] = source_features(sources(0))
    for i in range(n_tiles):
        generate(i)
    feat_j[...] = source_features(sources(1))
    red_ref[...] = reduce_rows(sources(0)).astype(BF)
    for i in range(n_tiles):
        combine(i)
        generate(i)
    feat_j[...] = source_features(sources(2))

    def pair(k, _):
        for b in (2 * k + 1, 2 * k + 2):
            fresh = source_features(sources(b + 2))
            rows = reduce_rows(sources(b)).astype(BF)
            for i in range(n_tiles):
                reduce(i)
                combine(i)
                generate(i)
            feat_j[...] = fresh
            red_ref[...] = rows
        return 0

    lax.fori_loop(0, n_blocks // 2, pair, 0)
    for i in range(n_tiles):
        reduce(i)
    for k in range(n_act):
        lanes = slice(k * 128, (k + 1) * 128)
        su = acc_u[:, lanes]
        sp = acc_p[:, lanes]
        st = active(k)
        near = sum(grid_split(st))
        at = near[0:3]
        accel = su[0:3] - at * su[6:7]
        jerk = su[3:6] - near[3:6] * su[6:7] - 3.0 * (sp[0:3] - at * sp[6:7])
        norm = jnp.sum(at * at, axis=0, keepdims=True) + soften_sq
        pot = 2.0 * jnp.sum(at * su[0:3], axis=0, keepdims=True) - su[7:8] - norm * su[6:7]
        out_ref[me ^ PARTNER[k]] = jnp.concatenate([accel, jerk, pot, jnp.zeros((1, 128), F32)], axis=0)


PARTNER = (0, 1, 2, 3, 6, 7, 4, 5)


def pair_sums(near, far, sources):
    n_act, n_src = 2 * near.shape[0], sources.shape[0]
    total = n_act * 128
    return pl.pallas_call(
        functools.partial(pair_kernel, n_src, n_act),
        out_shape=jax.ShapeDtypeStruct((n_act, 8, 128), F32),
        in_specs=[pl.BlockSpec(memory_space=pltpu.VMEM)] * 3,
        out_specs=pl.BlockSpec(memory_space=pltpu.VMEM),
        scratch_shapes=[
            pltpu.VMEM((8, n_src * 256 + 768), F32),
            pltpu.VMEM((256, 128), BF),
            pltpu.VMEM((n_act, 128, 128), BF),
            pltpu.VMEM((n_act, 128, 128), BF),
            pltpu.VMEM((32, 256), BF),
            pltpu.VMEM((8, total), F32),
            pltpu.VMEM((8, total), F32),
            *[pltpu.VMEM((256, 256), F32) for _ in range(2 * (total // 256))],
            *[pltpu.VMEM((4, 2, 256, 128), BF) for _ in range(total // 256)],
        ],
        name="pair_sums",
        cost_estimate=pl.CostEstimate(flops=400_000_000, bytes_accessed=400_000, transcendentals=8_000_000),
    )(near, far, sources)


def pick(table, slot):
    rows = []
    for k in range(table.shape[0] // 8):
        part = table[8 * k:8 * k + 8]
        low = jnp.broadcast_to(lax.rem(slot, 128), (8, 128))
        left = jnp.take_along_axis(part[:, 0:128], low, axis=1)
        right = jnp.take_along_axis(part[:, 128:256], low, axis=1)
        rows.append(jnp.where(slot < 128, left, right))
    return jnp.concatenate(rows, axis=0)


def predict_kernel(pos_ref, vel_ref, acc_ref, jerk_ref, mass_ref, level_ref, live_ref, slot_ref, src_ref, own_ref, act_ref):
    level = level_ref[...]
    half = jnp.where((level & 1) == 1, 0.5, 1.0)
    h = 0.5 * half * jnp.where((level & 2) == 2, 0.25, 1.0)
    acc, jerk, vel = acc_ref[...], jerk_ref[...], vel_ref[...]
    pos_pred = pos_ref[...] + h * (vel + h * (acc / 2.0 + h * jerk / 6.0))
    vel_pred = vel + h * (acc + h * jerk / 2.0)
    slots = lax.broadcasted_iota(jnp.int32, (1, 256), 1)
    count = live_ref[0]
    mass = jnp.where(slots < count, mass_ref[...], 0.0)
    counts = jnp.full((1, 256), count, jnp.int32).astype(F32)
    src = jnp.concatenate([pos_pred, vel_pred, mass, counts], axis=0)
    for k in range(src_ref.shape[0]):
        src_ref[k] = src
    rest = jnp.concatenate([acc, jerk, h, h], axis=0)
    own = pick(jnp.concatenate([src, rest], axis=0), slot_ref[...])
    own_ref[...] = own
    act_ref[0] = own[0:8]


def correct_kernel(own_ref, part_ref, state_ref, deriv_ref, pot_ref):
    summed = part_ref[0]
    for k in range(1, part_ref.shape[0]):
        summed = summed + part_ref[k]
    own = own_ref[...]
    pos_now, vel_now = own[0:3], own[3:6]
    acc_start, jerk_start, step = own[8:11], own[11:14], own[14:15]
    acc_end, jerk_end = summed[0:3], summed[3:6]
    differ = acc_start - acc_end
    fourth = -6.0 * differ - step * (4.0 * jerk_start + 2.0 * jerk_end)
    fifth = 12.0 * differ + 6.0 * step * (jerk_start + jerk_end)
    new_pos = pos_now + step * step / 24.0 * fourth + step * step / 120.0 * fifth
    new_vel = vel_now + step / 6.0 * fourth + step / 24.0 * fifth
    state_ref[...] = jnp.concatenate([new_pos, new_vel], axis=0)
    deriv_ref[...] = summed[0:6]
    pot_ref[...] = summed[6:7]


VM = pl.BlockSpec(memory_space=pltpu.VMEM)
SM = pl.BlockSpec(memory_space=pltpu.SMEM)
SRC_AXES = ("y", "z")
ACT_AXES = ("x", "c")


def shards(positions, velocities, accel_old, jerk_old, masses, levels, live_count, active_slot):
    n_src = 32
    src, own, act = pl.pallas_call(
        predict_kernel,
        out_shape=(
            jax.ShapeDtypeStruct((n_src, 8, 256), F32),
            jax.ShapeDtypeStruct((16, 128), F32),
            jax.ShapeDtypeStruct((1, 8, 128), F32),
        ),
        in_specs=[VM, VM, VM, VM, VM, VM, SM, VM],
        out_specs=(VM, VM, VM),
        name="predict",
    )(positions, velocities, accel_old, jerk_old, masses[None], levels[None], live_count, active_slot[None])
    sources = lax.all_to_all(src, SRC_AXES, 0, 0)
    two = jnp.concatenate([act, lax.ppermute(act, "c", ((0, 1), (1, 0)))])
    four = jnp.concatenate([two, lax.ppermute(two, "x", ((0, 1), (1, 0), (2, 3), (3, 2)))])
    far = lax.ppermute(four, "x", ((0, 3), (3, 0), (1, 2), (2, 1)))
    partial_sums = pair_sums(four, far, sources)
    parts = lax.all_to_all(partial_sums, ACT_AXES, 0, 0)
    state, deriv, pot = pl.pallas_call(
        correct_kernel,
        out_shape=(
            jax.ShapeDtypeStruct((6, 128), F32),
            jax.ShapeDtypeStruct((6, 128), F32),
            jax.ShapeDtypeStruct((1, 128), F32),
        ),
        in_specs=[VM, VM],
        out_specs=(VM, VM, VM),
        name="correct",
    )(own, parts)
    return state, deriv, pot[0]


def solution(mesh):
    fine = Mesh(mesh.devices.reshape(4, 4, 8, 2), ("x", "y", "z", "c"))
    every = ("x", "y", "z", "c")
    rows, flat = P(None, every), P(every)
    return jax.shard_map(
        shards,
        mesh=fine,
        in_specs=(rows, rows, rows, rows, flat, flat, flat, flat),
        out_specs=(rows, rows, flat),
        check_vma=False,
    )
```

time: 69.1 us -> 57.2 us (0.83); the launches traced: 68 us -> 56.8 us
  blocking collectives: 42.6 us -> 12.8 us
  starting transfers between devices: 0 us -> 16.9 us
  waiting for transfers between devices: 0 us -> 4.92 us
  Pallas kernels: 24.1 us -> 20.2 us
  local copies, waits for them, and re-layouts: 0 us -> 0.73 us
    all_to_all x2 -> x0, blocking collectives: 31.6 us -> none  [the longest x1 19.8 us: shards(): sources = lax.all_to_all(src, SRC_AXES, 0, 0)]
    all_to_all x0 -> x1, starting transfers between devices: none -> 12.2 us  [shards(): sources = lax.all_to_all(src, SRC_AXES, 0, 0)]
    ppermute x0 -> x3, starting transfers between devices: none -> 4.73 us  [the longest x1 2.48 us: shards(): far = lax.ppermute(four, 'x', ((0, 3), (3, 0), (1, 2), (2, 1)))]
    pallas_call x1, Pallas kernels: 21.2 us -> 17.3 us  [pair_sums(): pl.pallas_call(functools.partial(pair_kernel, n_src, n_act), out_shape=ja...]
    ppermute x0 -> x3, waiting for transfers between devices: none -> 3.72 us  [the longest x1 1.62 us: shards(): far = lax.ppermute(four, 'x', ((0, 3), (3, 0), (1, 2), (2, 1)))]
    all_to_all x1, blocking collectives: 11 us -> 12.8 us  [shards(): parts = lax.all_to_all(partial_sums, ACT_AXES, 0, 0)]
    all_to_all x0 -> x1, waiting for transfers between devices: none -> 1.2 us  [shards(): sources = lax.all_to_all(src, SRC_AXES, 0, 0)]
    unnamed x0 -> x10, local copies, waits for them, and re-layouts: none -> 0.73 us
  transfers between devices with their start and end apart: 0 -> 4, of which waited for: 0 -> 4; matrix products, arithmetic and copies ran while one was open for 0% -> 0% of each run, Pallas kernels for 0% -> 0%
where the time goes in v3:
time: 57.2 us; the launch traced here: 56.8 us
  Pallas kernels  20.2 us (35%)
  starting transfers between devices  16.9 us (30%)
  blocking collectives  12.8 us (22%)
  waiting for transfers between devices  4.92 us (9%)
  between operations  1.31 us (2%)
  local copies, waits for them, and re-layouts  0.73 us (1%)
    pallas_call x1, Pallas kernels, pair_sums(): pl.pallas_call(functools.partial(pair_kernel, n_src, n_act), out_shape=ja...  17.3 us
    all_to_all x1, blocking collectives, shards(): parts = lax.all_to_all(partial_sums, ACT_AXES, 0, 0)  12.8 us
    all_to_all x1, starting transfers between devices, shards(): sources = lax.all_to_all(src, SRC_AXES, 0, 0)  12.2 us
    ppermute x1, starting transfers between devices, shards(): far = lax.ppermute(four, 'x', ((0, 3), (3, 0), (1, 2), (2, 1)))  2.48 us
    ppermute x1, waiting for transfers between devices, shards(): far = lax.ppermute(four, 'x', ((0, 3), (3, 0), (1, 2), (2, 1)))  1.62 us
    pallas_call x1, Pallas kernels, shards(): pl.pallas_call(predict_kernel, out_shape=(jax.ShapeDtypeStruct((n_src, 8,...  1.51 us
    pallas_call x1, Pallas kernels, shards(): pl.pallas_call(correct_kernel, out_shape=(jax.ShapeDtypeStruct((6, 128),...  1.39 us
    ppermute x1, waiting for transfers between devices, shards(): lax.ppermute(two, 'x', ((0, 1), (1, 0), (2, 3), (3, 2)))  1.29 us
  transfers between devices with their start and end apart: 4, of which 4 were waited for; matrix products, arithmetic and copies ran while one was open for 0% of the time, Pallas kernels for 0%

profile of v3, /device:TPU:1, one launch (start us, length us, event | category | flops | bytes accessed | tf_op | source)
XLA Modules:
  0.0 56.8 jit_solution(2921227854911007629)
XLA Ops:
  1.3 1.5 %predict.1 = (f32[32,8,256]{2,1,0:T(8,128)}, f32[16,128]{1,0:T(8,128)}, f32[1,8,128]{2,1,0:T(8,128)}) custom-call(f32[3,256]{1,0:T(4,128)} %pos_ref.1, f32[3,256]{1,0:T(4,128)} %vel_ref.1, f32[3,256]{1,0:T(4,128)} %acc_ref.1, f32[3,256]{1,0:T(4,128)} %jerk_ref.1, f32[1,256]{1,0:T(1,128)} %bitcast.4, s32[1,256]{1,0:T(1,128)} %bitcast.5, s32[1]{0:T(128)S(6)} %copy.13.live_ref, ...), custom_call_target="tpu_custom_call" | custom-call | tf_op jit(solution)/shard_map/predict/pallas_call | solution.py:300
  2.8 0.0 copy-start.1
  2.8 12.2 %all-to-all-start = ((f32[32,8,256]{2,1,0:T(8,128)}), f32[32,8,256]{2,1,0:T(8,128)S(1)}, u32[]{:S(2)}, u32[]{:S(2)}) async-start(f32[32,8,256]{2,1,0:T(8,128)} %get-tuple-element.11), calls=%async_computation | async-start | bytes 524288 | tf_op jit(solution)/shard_map/all_to_all | solution.py:311
  15.0 0.0 copy-done.1
  15.0 1.0 %collective-permute-start = (f32[1,8,128]{2,1,0:T(8,128)S(1)}, f32[1,8,128]{2,1,0:T(8,128)S(1)}, u32[]{:S(2)}, u32[]{:S(2)}) collective-permute-start(f32[1,8,128]{2,1,0:T(8,128)S(1)} %copy-done.1), channel_id=1, source_target_pairs={{0,1},{1,0},{2,3},{3,2},{4,5},{5,4},{6,7},{7,6},{8,9},{9,8},{10,11... | collective-permute-start | bytes 12296 | tf_op jit(solution)/shard_map/ppermute | solution.py:312
  16.0 0.8 %collective-permute-done = f32[1,8,128]{2,1,0:T(8,128)S(1)} collective-permute-done((f32[1,8,128]{2,1,0:T(8,128)S(1)}, f32[1,8,128]{2,1,0:T(8,128)S(1)}, u32[]{:S(2)}, u32[]{:S(2)}) %collective-permute-start) | collective-permute-done | bytes 4128 | tf_op jit(solution)/shard_map/ppermute | solution.py:312
  16.8 1.2 %collective-permute-start.1 = (f32[2,8,128]{2,1,0:T(8,128)S(1)}, f32[2,8,128]{2,1,0:T(8,128)S(1)}, u32[]{:S(2)}, u32[]{:S(2)}) collective-permute-start(f32[2,8,128]{2,1,0:T(8,128)S(1)} %pad_maximum_fusion), channel_id=1, source_target_pairs={{0,64},{64,0},{128,192},{192,128},{1,65},{65,1},{129,193},{193,129... | collective-permute-start | bytes 24584 | tf_op jit(solution)/shard_map/ppermute | solution.py:313
  18.1 1.3 %collective-permute-done.1 = f32[2,8,128]{2,1,0:T(8,128)S(1)} collective-permute-done((f32[2,8,128]{2,1,0:T(8,128)S(1)}, f32[2,8,128]{2,1,0:T(8,128)S(1)}, u32[]{:S(2)}, u32[]{:S(2)}) %collective-permute-start.1) | collective-permute-done | bytes 8224 | tf_op jit(solution)/shard_map/ppermute | solution.py:313
  19.3 0.0 copy-start.2
  19.3 2.5 %collective-permute-start.2 = (f32[4,8,128]{2,1,0:T(8,128)S(1)}, f32[4,8,128]{2,1,0:T(8,128)S(1)}, u32[]{:S(2)}, u32[]{:S(2)}) collective-permute-start(f32[4,8,128]{2,1,0:T(8,128)S(1)} %constant_dynamic-update-slice_fusion.near_ref), channel_id=1, source_target_pairs={{0,192},{192,0},{64,128},{128,64},{1,193},{193,1},{65,129},{129,65... | collective-permute-start | bytes 49160 | tf_op jit(solution)/shard_map/ppermute | solution.py:314
  21.8 1.6 %collective-permute-done.2.far_ref = f32[4,8,128]{2,1,0:T(8,128)S(1)} collective-permute-done((f32[4,8,128]{2,1,0:T(8,128)S(1)}, f32[4,8,128]{2,1,0:T(8,128)S(1)}, u32[]{:S(2)}, u32[]{:S(2)}) %collective-permute-start.2) | collective-permute-done | bytes 16416 | tf_op jit(solution)/shard_map/ppermute | solution.py:314
  23.4 0.0 copy-start.3
  23.4 1.2 %all-to-all-done.src_ref = f32[32,8,256]{2,1,0:T(8,128)S(1)} async-done(((f32[32,8,256]{2,1,0:T(8,128)}), f32[32,8,256]{2,1,0:T(8,128)S(1)}, u32[]{:S(2)}, u32[]{:S(2)}) %all-to-all-start) | async-done | bytes 262176 | tf_op jit(solution)/shard_map/all_to_all | solution.py:311
  24.6 0.0 copy-done.2
  24.6 0.0 copy-done.3
  24.6 0.0 copy-start
  24.6 0.7 %copy-done = f32[32,8,256]{2,1,0:T(8,128)} copy-done((f32[32,8,256]{2,1,0:T(8,128)}, f32[32,8,256]{2,1,0:T(8,128)S(1)}, u32[]{:S(2)}) %copy-start) | copy-done | bytes 262168
  25.4 17.3 %pair_sums.1 = f32[8,8,128]{2,1,0:T(8,128)} custom-call(f32[4,8,128]{2,1,0:T(8,128)} %copy-done.2, f32[4,8,128]{2,1,0:T(8,128)} %copy-done.3, f32[32,8,256]{2,1,0:T(8,128)} %copy-done), custom_call_target="tpu_custom_call" | custom-call | flops 400000000 | bytes 400000 | tf_op jit(solution)/shard_map/pair_sums/pallas_call | solution.py:222
  42.6 12.8 %all_to_all.10.part_ref = f32[8,8,128]{2,1,0:T(8,128)} all-to-all(f32[8,8,128]{2,1,0:T(8,128)} %pair_sums.1), channel_id=1, replica_groups=mesh['x'=4,'y'=4,'z'=8,'c'=2] {'x','c'}, dimensions={0} | all-to-all | bytes 65536 | tf_op jit(solution)/shard_map/all_to_all | solution.py:316
  55.4 1.4 %correct.1 = (f32[6,128]{1,0:T(8,128)}, f32[6,128]{1,0:T(8,128)}, f32[1,128]{1,0:T(1,128)}) custom-call(f32[16,128]{1,0:T(8,128)} %get-tuple-element.9.own_ref, f32[8,8,128]{2,1,0:T(8,128)} %all_to_all.10.part_ref), custom_call_target="tpu_custom_call" | custom-call | tf_op jit(solution)/shard_map/correct/pallas_call | solution.py:317
  (4 shorter events, 0.0 us)
Async XLA Ops:
  2.8 12.2 %copy-start.1 = (f32[1,8,128]{2,1,0:T(8,128)S(1)}, f32[1,8,128]{2,1,0:T(8,128)}, u32[]{:S(2)}) copy-start(f32[1,8,128]{2,1,0:T(8,128)} %get-tuple-element.10) | copy-start | bytes 12292
  2.8 21.8 %all-to-all-start = ((f32[32,8,256]{2,1,0:T(8,128)}), f32[32,8,256]{2,1,0:T(8,128)S(1)}, u32[]{:S(2)}, u32[]{:S(2)}) async-start(f32[32,8,256]{2,1,0:T(8,128)} %get-tuple-element.11), calls=%async_computation | async-start | bytes 524288 | tf_op jit(solution)/shard_map/all_to_all | solution.py:311
  15.0 1.9 %collective-permute-start = (f32[1,8,128]{2,1,0:T(8,128)S(1)}, f32[1,8,128]{2,1,0:T(8,128)S(1)}, u32[]{:S(2)}, u32[]{:S(2)}) collective-permute-start(f32[1,8,128]{2,1,0:T(8,128)S(1)} %copy-done.1), channel_id=1, source_target_pairs={{0,1},{1,0},{2,3},{3,2},{4,5},{5,4},{6,7},{7,6},{8,9},{9,8},{10,11... | collective-permute-start | bytes 12296 | tf_op jit(solution)/shard_map/ppermute | solution.py:312
  16.8 2.5 %collective-permute-start.1 = (f32[2,8,128]{2,1,0:T(8,128)S(1)}, f32[2,8,128]{2,1,0:T(8,128)S(1)}, u32[]{:S(2)}, u32[]{:S(2)}) collective-permute-start(f32[2,8,128]{2,1,0:T(8,128)S(1)} %pad_maximum_fusion), channel_id=1, source_target_pairs={{0,64},{64,0},{128,192},{192,128},{1,65},{65,1},{129,193},{193,129... | collective-permute-start | bytes 24584 | tf_op jit(solution)/shard_map/ppermute | solution.py:313
  19.3 5.3 %copy-start.2 = (f32[4,8,128]{2,1,0:T(8,128)}, f32[4,8,128]{2,1,0:T(8,128)S(1)}, u32[]{:S(2)}) copy-start(f32[4,8,128]{2,1,0:T(8,128)S(1)} %constant_dynamic-update-slice_fusion.near_ref) | copy-start | bytes 49156
  19.3 4.1 %collective-permute-start.2 = (f32[4,8,128]{2,1,0:T(8,128)S(1)}, f32[4,8,128]{2,1,0:T(8,128)S(1)}, u32[]{:S(2)}, u32[]{:S(2)}) collective-permute-start(f32[4,8,128]{2,1,0:T(8,128)S(1)} %constant_dynamic-update-slice_fusion.near_ref), channel_id=1, source_target_pairs={{0,192},{192,0},{64,128},{128,64},{1,193},{193,1},{65,129},{129,65... | collective-permute-start | bytes 49160 | tf_op jit(solution)/shard_map/ppermute | solution.py:314
  23.4 1.2 %copy-start.3 = (f32[4,8,128]{2,1,0:T(8,128)}, f32[4,8,128]{2,1,0:T(8,128)S(1)}, u32[]{:S(2)}) copy-start(f32[4,8,128]{2,1,0:T(8,128)S(1)} %collective-permute-done.2.far_ref) | copy-start | bytes 49156
  24.6 0.7 %copy-start = (f32[32,8,256]{2,1,0:T(8,128)}, f32[32,8,256]{2,1,0:T(8,128)S(1)}, u32[]{:S(2)}) copy-start(f32[32,8,256]{2,1,0:T(8,128)S(1)} %all-to-all-done.src_ref) | copy-start | bytes 786436

commit v4 on v3

--- a/solution.py
+++ b/solution.py
@@ -9,6 +9,10 @@
 soften_sq = 0.0001
 BF = jnp.bfloat16
 F32 = jnp.float32
+
+
+def in_vmem(x):
+    return pltpu.with_memory_space_constraint(x, pltpu.VMEM)
 
 
 def round_bf(x):
@@ -111,23 +115,21 @@
         return near_ref[k] if k < n_act // 2 else far_ref[k - n_act // 2]
 
     q_bufs, d_bufs, v_bufs = (bufs[k * n_tiles:(k + 1) * n_tiles] for k in range(3))
-    width = n_src * 256 + 768
-    for t in range(width // 128):
-        dense[:, t * 128:(t + 1) * 128] = jnp.zeros((8, 128), F32)
+    dense[...] = jnp.zeros_like(dense)
     lane = lax.broadcasted_iota(jnp.int32, (8, 128), 1)
     counts = [jnp.max(src_ref[b, 7:8, 0:128]).astype(jnp.int32) for b in range(n_src)]
     offset = jnp.int32(0)
     for b in range(n_src):
-        shift = lax.rem(offset, 128)
-        start = pl.multiple_of(offset - shift, 128)
+        shift = offset & 127
+        at = offset >> 7
         left = pltpu.roll(src_ref[b, :, 0:128], shift, 1)
         right = pltpu.roll(src_ref[b, :, 128:256], shift, 1)
         before = lane < shift
-        dense[:, pl.ds(start, 128)] = jnp.where(before, dense[:, pl.ds(start, 128)], left)
-        dense[:, pl.ds(start + 128, 128)] = jnp.where(before, left, right)
-        dense[:, pl.ds(start + 256, 128)] = jnp.where(before, right, 0.0)
+        dense[at] = jnp.where(before, dense[at], left)
+        dense[at + 1] = jnp.where(before, left, right)
+        dense[at + 2] = jnp.where(before, right, 0.0)
         offset = offset + counts[b]
-    n_blocks = (offset + (tile - 1)) // tile
+    n_blocks = (offset + (tile - 1)) >> 8
     for k in range(n_act):
         fq, fd = active_features(active(k))
         feat_q[k] = fq.astype(BF)
@@ -136,7 +138,7 @@
     acc_p[...] = jnp.zeros_like(acc_p)
 
     def sources(b):
-        return dense[:, pl.ds(pl.multiple_of(b * tile, tile), tile)]
+        return jnp.concatenate([dense[2 * b], dense[2 * b + 1]], axis=1)
 
     def wide(ref, *at):
         return jnp.concatenate([ref[(*at, 0)], ref[(*at, 1)]], axis=1)
@@ -221,11 +223,11 @@
     total = n_act * 128
     return pl.pallas_call(
         functools.partial(pair_kernel, n_src, n_act),
-        out_shape=jax.ShapeDtypeStruct((n_act, 8, 128), F32),
+        out_shape=pltpu.VMEM((n_act, 8, 128), F32),
         in_specs=[pl.BlockSpec(memory_space=pltpu.VMEM)] * 3,
         out_specs=pl.BlockSpec(memory_space=pltpu.VMEM),
         scratch_shapes=[
-            pltpu.VMEM((8, n_src * 256 + 768), F32),
+            pltpu.VMEM((2 * n_src + 6, 8, 128), F32),
             pltpu.VMEM((256, 128), BF),
             pltpu.VMEM((n_act, 128, 128), BF),
             pltpu.VMEM((n_act, 128, 128), BF),
@@ -237,7 +239,7 @@
         ],
         name="pair_sums",
         cost_estimate=pl.CostEstimate(flops=400_000_000, bytes_accessed=400_000, transcendentals=8_000_000),
-    )(near, far, sources)
+    )(*map(in_vmem, (near, far, sources)))
 
 
 def pick(table, slot):
@@ -300,9 +302,9 @@
     src, own, act = pl.pallas_call(
         predict_kernel,
         out_shape=(
-            jax.ShapeDtypeStruct((n_src, 8, 256), F32),
-            jax.ShapeDtypeStruct((16, 128), F32),
-            jax.ShapeDtypeStruct((1, 8, 128), F32),
+            pltpu.VMEM((n_src, 8, 256), F32),
+            pltpu.VMEM((16, 128), F32),
+            pltpu.VMEM((1, 8, 128), F32),
         ),
         in_specs=[VM, VM, VM, VM, VM, VM, SM, VM],
         out_specs=(VM, VM, VM),
@@ -324,7 +326,7 @@
         in_specs=[VM, VM],
         out_specs=(VM, VM, VM),
         name="correct",
-    )(own, parts)
+    )(in_vmem(own), in_vmem(parts))
     return state, deriv, pot[0]
 
 

time: 57.2 us -> 52.9 us (0.925); the launches traced: 56.8 us -> 53.2 us
  Pallas kernels: 20.2 us -> 17.7 us
  local copies, waits for them, and re-layouts: 0.73 us -> 0.01 us
    pallas_call x2, Pallas kernels: 18.8 us -> 17.1 us  [the longest x1 15.6 us: pair_sums(): pl.pallas_call(functools.partial(pair_kernel, n_src, n_act), out_shape=pl...]
    pallas_call x1, Pallas kernels: 1.39 us -> 0.61 us  [shards(): pl.pallas_call(correct_kernel, out_shape=(jax.ShapeDtypeStruct((6, 128),...]
    unnamed x10 -> x2, local copies, waits for them, and re-layouts: 0.73 us -> 0.01 us
where the time goes in v4:
time: 52.9 us; the launch traced here: 53.2 us
  Pallas kernels  17.7 us (33%)
  starting transfers between devices  16.8 us (32%)
  blocking collectives  12.5 us (24%)
  waiting for transfers between devices  4.94 us (9%)
  between operations  1.3 us (2%)
    pallas_call x1, Pallas kernels, pair_sums(): pl.pallas_call(functools.partial(pair_kernel, n_src, n_act), out_shape=pl...  15.6 us
    all_to_all x1, blocking collectives, shards(): parts = lax.all_to_all(partial_sums, ACT_AXES, 0, 0)  12.5 us
    all_to_all x1, starting transfers between devices, shards(): sources = lax.all_to_all(src, SRC_AXES, 0, 0)  12 us
    ppermute x1, starting transfers between devices, shards(): far = lax.ppermute(four, 'x', ((0, 3), (3, 0), (1, 2), (2, 1)))  2.48 us
    ppermute x1, waiting for transfers between devices, shards(): far = lax.ppermute(four, 'x', ((0, 3), (3, 0), (1, 2), (2, 1)))  1.62 us
    pallas_call x1, Pallas kernels, shards(): pl.pallas_call(predict_kernel, out_shape=(pltpu.VMEM((n_src, 8, 256), F32...  1.5 us
    ppermute x1, waiting for transfers between devices, shards(): lax.ppermute(two, 'x', ((0, 1), (1, 0), (2, 3), (3, 2)))  1.29 us
    all_to_all x1, waiting for transfers between devices, shards(): sources = lax.all_to_all(src, SRC_AXES, 0, 0)  1.21 us
  transfers between devices with their start and end apart: 4, of which 4 were waited for; matrix products, arithmetic and copies ran while one was open for 0% of the time, Pallas kernels for 0%

profile of v4, /device:TPU:1, one launch (start us, length us, event | category | flops | bytes accessed | tf_op | source)
XLA Modules:
  0.0 53.2 jit_solution(6261744066444329170)
XLA Ops:
  1.3 1.5 %predict.1 = (f32[32,8,256]{2,1,0:T(8,128)}, f32[16,128]{1,0:T(8,128)S(1)}, f32[1,8,128]{2,1,0:T(8,128)S(1)}) custom-call(f32[3,256]{1,0:T(4,128)} %pos_ref.1, f32[3,256]{1,0:T(4,128)} %vel_ref.1, f32[3,256]{1,0:T(4,128)} %acc_ref.1, f32[3,256]{1,0:T(4,128)} %jerk_ref.1, f32[1,256]{1,0:T(1,128)} %bitcast.4, s32[1,256]{1,0:T(1,128)} %bitcast.5, ...), custom_call_target="tpu_custom_call" | custom-call | tf_op jit(solution)/shard_map/predict/pallas_call | solution.py:302
  2.8 12.0 %all-to-all-start = ((f32[32,8,256]{2,1,0:T(8,128)}), f32[32,8,256]{2,1,0:T(8,128)S(1)}, u32[]{:S(2)}, u32[]{:S(2)}) async-start(f32[32,8,256]{2,1,0:T(8,128)} %get-tuple-element.11), calls=%async_computation | async-start | bytes 524288 | tf_op jit(solution)/shard_map/all_to_all | solution.py:313
  14.8 1.0 %collective-permute-start = (f32[1,8,128]{2,1,0:T(8,128)S(1)}, f32[1,8,128]{2,1,0:T(8,128)S(1)}, u32[]{:S(2)}, u32[]{:S(2)}) collective-permute-start(f32[1,8,128]{2,1,0:T(8,128)S(1)} %get-tuple-element.10), channel_id=1, source_target_pairs={{0,1},{1,0},{2,3},{3,2},{4,5},{5,4},{6,7},{7,6},{8,9},{9,8},{10,11... | collective-permute-start | bytes 12296 | tf_op jit(solution)/shard_map/ppermute | solution.py:314
  15.9 0.8 %collective-permute-done = f32[1,8,128]{2,1,0:T(8,128)S(1)} collective-permute-done((f32[1,8,128]{2,1,0:T(8,128)S(1)}, f32[1,8,128]{2,1,0:T(8,128)S(1)}, u32[]{:S(2)}, u32[]{:S(2)}) %collective-permute-start) | collective-permute-done | bytes 4128 | tf_op jit(solution)/shard_map/ppermute | solution.py:314
  16.7 1.2 %collective-permute-start.1 = (f32[2,8,128]{2,1,0:T(8,128)S(1)}, f32[2,8,128]{2,1,0:T(8,128)S(1)}, u32[]{:S(2)}, u32[]{:S(2)}) collective-permute-start(f32[2,8,128]{2,1,0:T(8,128)S(1)} %pad_maximum_fusion), channel_id=1, source_target_pairs={{0,64},{64,0},{128,192},{192,128},{1,65},{65,1},{129,193},{193,129... | collective-permute-start | bytes 24584 | tf_op jit(solution)/shard_map/ppermute | solution.py:315
  17.9 1.3 %collective-permute-done.1 = f32[2,8,128]{2,1,0:T(8,128)S(1)} collective-permute-done((f32[2,8,128]{2,1,0:T(8,128)S(1)}, f32[2,8,128]{2,1,0:T(8,128)S(1)}, u32[]{:S(2)}, u32[]{:S(2)}) %collective-permute-start.1) | collective-permute-done | bytes 8224 | tf_op jit(solution)/shard_map/ppermute | solution.py:315
  19.2 2.5 %collective-permute-start.2 = (f32[4,8,128]{2,1,0:T(8,128)S(1)}, f32[4,8,128]{2,1,0:T(8,128)S(1)}, u32[]{:S(2)}, u32[]{:S(2)}) collective-permute-start(f32[4,8,128]{2,1,0:T(8,128)S(1)} %constant_dynamic-update-slice_fusion.near_ref), channel_id=1, source_target_pairs={{0,192},{192,0},{64,128},{128,64},{1,193},{193,1},{65,129},{129,65... | collective-permute-start | bytes 49160 | tf_op jit(solution)/shard_map/ppermute | solution.py:316
  21.7 1.6 %collective-permute-done.2.far_ref = f32[4,8,128]{2,1,0:T(8,128)S(1)} collective-permute-done((f32[4,8,128]{2,1,0:T(8,128)S(1)}, f32[4,8,128]{2,1,0:T(8,128)S(1)}, u32[]{:S(2)}, u32[]{:S(2)}) %collective-permute-start.2) | collective-permute-done | bytes 16416 | tf_op jit(solution)/shard_map/ppermute | solution.py:316
  23.3 1.2 %all-to-all-done.src_ref = f32[32,8,256]{2,1,0:T(8,128)S(1)} async-done(((f32[32,8,256]{2,1,0:T(8,128)}), f32[32,8,256]{2,1,0:T(8,128)S(1)}, u32[]{:S(2)}, u32[]{:S(2)}) %all-to-all-start) | async-done | bytes 262176 | tf_op jit(solution)/shard_map/all_to_all | solution.py:313
  24.5 15.6 %pair_sums.1 = f32[8,8,128]{2,1,0:T(8,128)S(1)} custom-call(f32[4,8,128]{2,1,0:T(8,128)S(1)} %constant_dynamic-update-slice_fusion.near_ref, f32[4,8,128]{2,1,0:T(8,128)S(1)} %collective-permute-done.2.far_ref, f32[32,8,256]{2,1,0:T(8,128)S(1)} %all-to-all-done.src_ref), custom_call_target="tpu_custom_call" | custom-call | flops 400000000 | bytes 400000 | tf_op jit(solution)/shard_map/pair_sums/pallas_call | solution.py:224
  40.1 12.5 %all_to_all.10.part_ref = f32[8,8,128]{2,1,0:T(8,128)S(1)} all-to-all(f32[8,8,128]{2,1,0:T(8,128)S(1)} %pair_sums.1), channel_id=1, replica_groups=mesh['x'=4,'y'=4,'z'=8,'c'=2] {'x','c'}, dimensions={0} | all-to-all | bytes 65536 | tf_op jit(solution)/shard_map/all_to_all | solution.py:318
  52.6 0.6 %correct.1 = (f32[6,128]{1,0:T(8,128)}, f32[6,128]{1,0:T(8,128)}, f32[1,128]{1,0:T(1,128)}) custom-call(f32[16,128]{1,0:T(8,128)S(1)} %get-tuple-element.9.own_ref, f32[8,8,128]{2,1,0:T(8,128)S(1)} %all_to_all.10.part_ref), custom_call_target="tpu_custom_call" | custom-call | tf_op jit(solution)/shard_map/correct/pallas_call | solution.py:319
  (4 shorter events, 0.0 us)
Async XLA Ops:
  2.8 21.7 %all-to-all-start = ((f32[32,8,256]{2,1,0:T(8,128)}), f32[32,8,256]{2,1,0:T(8,128)S(1)}, u32[]{:S(2)}, u32[]{:S(2)}) async-start(f32[32,8,256]{2,1,0:T(8,128)} %get-tuple-element.11), calls=%async_computation | async-start | bytes 524288 | tf_op jit(solution)/shard_map/all_to_all | solution.py:313
  14.8 1.9 %collective-permute-start = (f32[1,8,128]{2,1,0:T(8,128)S(1)}, f32[1,8,128]{2,1,0:T(8,128)S(1)}, u32[]{:S(2)}, u32[]{:S(2)}) collective-permute-start(f32[1,8,128]{2,1,0:T(8,128)S(1)} %get-tuple-element.10), channel_id=1, source_target_pairs={{0,1},{1,0},{2,3},{3,2},{4,5},{5,4},{6,7},{7,6},{8,9},{9,8},{10,11... | collective-permute-start | bytes 12296 | tf_op jit(solution)/shard_map/ppermute | solution.py:314
  16.7 2.5 %collective-permute-start.1 = (f32[2,8,128]{2,1,0:T(8,128)S(1)}, f32[2,8,128]{2,1,0:T(8,128)S(1)}, u32[]{:S(2)}, u32[]{:S(2)}) collective-permute-start(f32[2,8,128]{2,1,0:T(8,128)S(1)} %pad_maximum_fusion), channel_id=1, source_target_pairs={{0,64},{64,0},{128,192},{192,128},{1,65},{65,1},{129,193},{193,129... | collective-permute-start | bytes 24584 | tf_op jit(solution)/shard_map/ppermute | solution.py:315
  19.2 4.1 %collective-permute-start.2 = (f32[4,8,128]{2,1,0:T(8,128)S(1)}, f32[4,8,128]{2,1,0:T(8,128)S(1)}, u32[]{:S(2)}, u32[]{:S(2)}) collective-permute-start(f32[4,8,128]{2,1,0:T(8,128)S(1)} %constant_dynamic-update-slice_fusion.near_ref), channel_id=1, source_target_pairs={{0,192},{192,0},{64,128},{128,64},{1,193},{193,1},{65,129},{129,65... | collective-permute-start | bytes 49160 | tf_op jit(solution)/shard_map/ppermute | solution.py:316

commit v5 on v4

--- a/solution.py
+++ b/solution.py
@@ -186,19 +186,26 @@
         generate(i)
     feat_j[...] = source_features(sources(2))
 
-    def pair(k, _):
-        for b in (2 * k + 1, 2 * k + 2):
-            fresh = source_features(sources(b + 2))
-            rows = reduce_rows(sources(b)).astype(BF)
-            for i in range(n_tiles):
-                reduce(i)
-                combine(i)
-                generate(i)
-            feat_j[...] = fresh
-            red_ref[...] = rows
-        return 0
-
-    lax.fori_loop(0, n_blocks // 2, pair, 0)
+    def several(first, count):
+        def body(k, _):
+            for j in range(count):
+                b = first + count * k + j
+                fresh = source_features(sources(b + 2))
+                rows = reduce_rows(sources(b)).astype(BF)
+                for i in range(n_tiles):
+                    reduce(i)
+                    combine(i)
+                    generate(i)
+                feat_j[...] = fresh
+                red_ref[...] = rows
+            return 0
+
+        return body
+
+    rest = n_blocks - 1
+    lax.fori_loop(0, rest >> 2, several(1, 4), 0)
+    lax.fori_loop(0, (rest >> 1) & 1, several(1 + (rest & -4), 2), 0)
+    lax.fori_loop(0, rest & 1, several(1 + (rest & -2), 1), 0)
     for i in range(n_tiles):
         reduce(i)
     for k in range(n_act):

time: 52.9 us -> 52.4 us (level); the launches traced: 53.2 us -> 51.9 us
  Pallas kernels: 17.7 us -> 15.6 us
  blocking collectives: 12.5 us -> 13.2 us
    pallas_call x1, Pallas kernels: 15.6 us -> 13.5 us  [pair_sums(): pl.pallas_call(functools.partial(pair_kernel, n_src, n_act), out_shape=pl...]
    all_to_all x1, blocking collectives: 12.5 us -> 13.2 us  [shards(): parts = lax.all_to_all(partial_sums, ACT_AXES, 0, 0)]
where the time goes in v5:
time: 52.4 us; the launch traced here: 51.9 us
  starting transfers between devices  16.8 us (32%)
  Pallas kernels  15.6 us (30%)
  blocking collectives  13.2 us (25%)
  waiting for transfers between devices  4.94 us (9%)
  between operations  1.3 us (2%)
    pallas_call x1, Pallas kernels, pair_sums(): pl.pallas_call(functools.partial(pair_kernel, n_src, n_act), out_shape=pl...  13.5 us
    all_to_all x1, blocking collectives, shards(): parts = lax.all_to_all(partial_sums, ACT_AXES, 0, 0)  13.2 us
    all_to_all x1, starting transfers between devices, shards(): sources = lax.all_to_all(src, SRC_AXES, 0, 0)  12 us
    ppermute x1, starting transfers between devices, shards(): far = lax.ppermute(four, 'x', ((0, 3), (3, 0), (1, 2), (2, 1)))  2.48 us
    ppermute x1, waiting for transfers between devices, shards(): far = lax.ppermute(four, 'x', ((0, 3), (3, 0), (1, 2), (2, 1)))  1.62 us
    pallas_call x1, Pallas kernels, shards(): pl.pallas_call(predict_kernel, out_shape=(pltpu.VMEM((n_src, 8, 256), F32...  1.5 us
    ppermute x1, waiting for transfers between devices, shards(): lax.ppermute(two, 'x', ((0, 1), (1, 0), (2, 3), (3, 2)))  1.29 us
    all_to_all x1, waiting for transfers between devices, shards(): sources = lax.all_to_all(src, SRC_AXES, 0, 0)  1.21 us
  transfers between devices with their start and end apart: 4, of which 4 were waited for; matrix products, arithmetic and copies ran while one was open for 0% of the time, Pallas kernels for 0%

profile of v5, /device:TPU:1, one launch (start us, length us, event | category | flops | bytes accessed | tf_op | source)
XLA Modules:
  0.0 51.9 jit_solution(7737848889611963664)
XLA Ops:
  1.3 1.5 %predict.1 = (f32[32,8,256]{2,1,0:T(8,128)}, f32[16,128]{1,0:T(8,128)S(1)}, f32[1,8,128]{2,1,0:T(8,128)S(1)}) custom-call(f32[3,256]{1,0:T(4,128)} %pos_ref.1, f32[3,256]{1,0:T(4,128)} %vel_ref.1, f32[3,256]{1,0:T(4,128)} %acc_ref.1, f32[3,256]{1,0:T(4,128)} %jerk_ref.1, f32[1,256]{1,0:T(1,128)} %bitcast.4, s32[1,256]{1,0:T(1,128)} %bitcast.5, ...), custom_call_target="tpu_custom_call" | custom-call | tf_op jit(solution)/shard_map/predict/pallas_call | solution.py:309
  2.8 12.0 %all-to-all-start = ((f32[32,8,256]{2,1,0:T(8,128)}), f32[32,8,256]{2,1,0:T(8,128)S(1)}, u32[]{:S(2)}, u32[]{:S(2)}) async-start(f32[32,8,256]{2,1,0:T(8,128)} %get-tuple-element.11), calls=%async_computation | async-start | bytes 524288 | tf_op jit(solution)/shard_map/all_to_all | solution.py:320
  14.8 1.0 %collective-permute-start = (f32[1,8,128]{2,1,0:T(8,128)S(1)}, f32[1,8,128]{2,1,0:T(8,128)S(1)}, u32[]{:S(2)}, u32[]{:S(2)}) collective-permute-start(f32[1,8,128]{2,1,0:T(8,128)S(1)} %get-tuple-element.10), channel_id=1, source_target_pairs={{0,1},{1,0},{2,3},{3,2},{4,5},{5,4},{6,7},{7,6},{8,9},{9,8},{10,11... | collective-permute-start | bytes 12296 | tf_op jit(solution)/shard_map/ppermute | solution.py:321
  15.9 0.8 %collective-permute-done = f32[1,8,128]{2,1,0:T(8,128)S(1)} collective-permute-done((f32[1,8,128]{2,1,0:T(8,128)S(1)}, f32[1,8,128]{2,1,0:T(8,128)S(1)}, u32[]{:S(2)}, u32[]{:S(2)}) %collective-permute-start) | collective-permute-done | bytes 4128 | tf_op jit(solution)/shard_map/ppermute | solution.py:321
  16.7 1.2 %collective-permute-start.1 = (f32[2,8,128]{2,1,0:T(8,128)S(1)}, f32[2,8,128]{2,1,0:T(8,128)S(1)}, u32[]{:S(2)}, u32[]{:S(2)}) collective-permute-start(f32[2,8,128]{2,1,0:T(8,128)S(1)} %pad_maximum_fusion), channel_id=1, source_target_pairs={{0,64},{64,0},{128,192},{192,128},{1,65},{65,1},{129,193},{193,129... | collective-permute-start | bytes 24584 | tf_op jit(solution)/shard_map/ppermute | solution.py:322
  17.9 1.3 %collective-permute-done.1 = f32[2,8,128]{2,1,0:T(8,128)S(1)} collective-permute-done((f32[2,8,128]{2,1,0:T(8,128)S(1)}, f32[2,8,128]{2,1,0:T(8,128)S(1)}, u32[]{:S(2)}, u32[]{:S(2)}) %collective-permute-start.1) | collective-permute-done | bytes 8224 | tf_op jit(solution)/shard_map/ppermute | solution.py:322
  19.2 2.5 %collective-permute-start.2 = (f32[4,8,128]{2,1,0:T(8,128)S(1)}, f32[4,8,128]{2,1,0:T(8,128)S(1)}, u32[]{:S(2)}, u32[]{:S(2)}) collective-permute-start(f32[4,8,128]{2,1,0:T(8,128)S(1)} %constant_dynamic-update-slice_fusion.near_ref), channel_id=1, source_target_pairs={{0,192},{192,0},{64,128},{128,64},{1,193},{193,1},{65,129},{129,65... | collective-permute-start | bytes 49160 | tf_op jit(solution)/shard_map/ppermute | solution.py:323
  21.7 1.6 %collective-permute-done.2.far_ref = f32[4,8,128]{2,1,0:T(8,128)S(1)} collective-permute-done((f32[4,8,128]{2,1,0:T(8,128)S(1)}, f32[4,8,128]{2,1,0:T(8,128)S(1)}, u32[]{:S(2)}, u32[]{:S(2)}) %collective-permute-start.2) | collective-permute-done | bytes 16416 | tf_op jit(solution)/shard_map/ppermute | solution.py:323
  23.3 1.2 %all-to-all-done.src_ref = f32[32,8,256]{2,1,0:T(8,128)S(1)} async-done(((f32[32,8,256]{2,1,0:T(8,128)}), f32[32,8,256]{2,1,0:T(8,128)S(1)}, u32[]{:S(2)}, u32[]{:S(2)}) %all-to-all-start) | async-done | bytes 262176 | tf_op jit(solution)/shard_map/all_to_all | solution.py:320
  24.5 13.5 %pair_sums.1 = f32[8,8,128]{2,1,0:T(8,128)S(1)} custom-call(f32[4,8,128]{2,1,0:T(8,128)S(1)} %constant_dynamic-update-slice_fusion.near_ref, f32[4,8,128]{2,1,0:T(8,128)S(1)} %collective-permute-done.2.far_ref, f32[32,8,256]{2,1,0:T(8,128)S(1)} %all-to-all-done.src_ref), custom_call_target="tpu_custom_call" | custom-call | flops 400000000 | bytes 400000 | tf_op jit(solution)/shard_map/pair_sums/pallas_call | solution.py:231
  38.0 13.2 %all_to_all.10.part_ref = f32[8,8,128]{2,1,0:T(8,128)S(1)} all-to-all(f32[8,8,128]{2,1,0:T(8,128)S(1)} %pair_sums.1), channel_id=1, replica_groups=mesh['x'=4,'y'=4,'z'=8,'c'=2] {'x','c'}, dimensions={0} | all-to-all | bytes 65536 | tf_op jit(solution)/shard_map/all_to_all | solution.py:325
  51.2 0.6 %correct.1 = (f32[6,128]{1,0:T(8,128)}, f32[6,128]{1,0:T(8,128)}, f32[1,128]{1,0:T(1,128)}) custom-call(f32[16,128]{1,0:T(8,128)S(1)} %get-tuple-element.9.own_ref, f32[8,8,128]{2,1,0:T(8,128)S(1)} %all_to_all.10.part_ref), custom_call_target="tpu_custom_call" | custom-call | tf_op jit(solution)/shard_map/correct/pallas_call | solution.py:326
  (4 shorter events, 0.0 us)
Async XLA Ops:
  2.8 21.7 %all-to-all-start = ((f32[32,8,256]{2,1,0:T(8,128)}), f32[32,8,256]{2,1,0:T(8,128)S(1)}, u32[]{:S(2)}, u32[]{:S(2)}) async-start(f32[32,8,256]{2,1,0:T(8,128)} %get-tuple-element.11), calls=%async_computation | async-start | bytes 524288 | tf_op jit(solution)/shard_map/all_to_all | solution.py:320
  14.8 1.9 %collective-permute-start = (f32[1,8,128]{2,1,0:T(8,128)S(1)}, f32[1,8,128]{2,1,0:T(8,128)S(1)}, u32[]{:S(2)}, u32[]{:S(2)}) collective-permute-start(f32[1,8,128]{2,1,0:T(8,128)S(1)} %get-tuple-element.10), channel_id=1, source_target_pairs={{0,1},{1,0},{2,3},{3,2},{4,5},{5,4},{6,7},{7,6},{8,9},{9,8},{10,11... | collective-permute-start | bytes 12296 | tf_op jit(solution)/shard_map/ppermute | solution.py:321
  16.7 2.5 %collective-permute-start.1 = (f32[2,8,128]{2,1,0:T(8,128)S(1)}, f32[2,8,128]{2,1,0:T(8,128)S(1)}, u32[]{:S(2)}, u32[]{:S(2)}) collective-permute-start(f32[2,8,128]{2,1,0:T(8,128)S(1)} %pad_maximum_fusion), channel_id=1, source_target_pairs={{0,64},{64,0},{128,192},{192,128},{1,65},{65,1},{129,193},{193,129... | collective-permute-start | bytes 24584 | tf_op jit(solution)/shard_map/ppermute | solution.py:322
  19.2 4.1 %collective-permute-start.2 = (f32[4,8,128]{2,1,0:T(8,128)S(1)}, f32[4,8,128]{2,1,0:T(8,128)S(1)}, u32[]{:S(2)}, u32[]{:S(2)}) collective-permute-start(f32[4,8,128]{2,1,0:T(8,128)S(1)} %constant_dynamic-update-slice_fusion.near_ref), channel_id=1, source_target_pairs={{0,192},{192,0},{64,128},{128,64},{1,193},{193,1},{65,129},{129,65... | collective-permute-start | bytes 49160 | tf_op jit(solution)/shard_map/ppermute | solution.py:323

commit v6 on v5

--- a/solution.py
+++ b/solution.py
@@ -202,10 +202,15 @@
 
         return body
 
-    rest = n_blocks - 1
+    rest = jnp.maximum(n_blocks - 2, 0)
     lax.fori_loop(0, rest >> 2, several(1, 4), 0)
     lax.fori_loop(0, (rest >> 1) & 1, several(1 + (rest & -4), 2), 0)
     lax.fori_loop(0, rest & 1, several(1 + (rest & -2), 1), 0)
+    rows = reduce_rows(sources(jnp.maximum(n_blocks - 1, 1))).astype(BF)
+    for i in range(n_tiles):
+        reduce(i)
+        combine(i)
+    red_ref[...] = rows
     for i in range(n_tiles):
         reduce(i)
     for k in range(n_act):

time: 52.4 us -> 51.9 us (level)
  no operation moved by 1% of the time
where the time goes in v6:
time: 51.9 us; the launch traced here: 51.6 us
  starting transfers between devices  16.8 us (32%)
  Pallas kernels  15.7 us (30%)
  blocking collectives  12.9 us (25%)
  waiting for transfers between devices  4.94 us (10%)
  between operations  1.3 us (3%)
    pallas_call x1, Pallas kernels, pair_sums(): pl.pallas_call(functools.partial(pair_kernel, n_src, n_act), out_shape=pl...  13.5 us
    all_to_all x1, blocking collectives, shards(): parts = lax.all_to_all(partial_sums, ACT_AXES, 0, 0)  12.9 us
    all_to_all x1, starting transfers between devices, shards(): sources = lax.all_to_all(src, SRC_AXES, 0, 0)  12 us
    ppermute x1, starting transfers between devices, shards(): far = lax.ppermute(four, 'x', ((0, 3), (3, 0), (1, 2), (2, 1)))  2.48 us
    ppermute x1, waiting for transfers between devices, shards(): far = lax.ppermute(four, 'x', ((0, 3), (3, 0), (1, 2), (2, 1)))  1.62 us
    pallas_call x1, Pallas kernels, shards(): pl.pallas_call(predict_kernel, out_shape=(pltpu.VMEM((n_src, 8, 256), F32...  1.5 us
    ppermute x1, waiting for transfers between devices, shards(): lax.ppermute(two, 'x', ((0, 1), (1, 0), (2, 3), (3, 2)))  1.29 us
    all_to_all x1, waiting for transfers between devices, shards(): sources = lax.all_to_all(src, SRC_AXES, 0, 0)  1.21 us
  transfers between devices with their start and end apart: 4, of which 4 were waited for; matrix products, arithmetic and copies ran while one was open for 0% of the time, Pallas kernels for 0%

profile of v6, /device:TPU:1, one launch (start us, length us, event | category | flops | bytes accessed | tf_op | source)
XLA Modules:
  0.0 51.6 jit_solution(4650091375074072526)
XLA Ops:
  1.3 1.5 %predict.1 = (f32[32,8,256]{2,1,0:T(8,128)}, f32[16,128]{1,0:T(8,128)S(1)}, f32[1,8,128]{2,1,0:T(8,128)S(1)}) custom-call(f32[3,256]{1,0:T(4,128)} %pos_ref.1, f32[3,256]{1,0:T(4,128)} %vel_ref.1, f32[3,256]{1,0:T(4,128)} %acc_ref.1, f32[3,256]{1,0:T(4,128)} %jerk_ref.1, f32[1,256]{1,0:T(1,128)} %bitcast.4, s32[1,256]{1,0:T(1,128)} %bitcast.5, ...), custom_call_target="tpu_custom_call" | custom-call | tf_op jit(solution)/shard_map/predict/pallas_call | solution.py:314
  2.8 12.0 %all-to-all-start = ((f32[32,8,256]{2,1,0:T(8,128)}), f32[32,8,256]{2,1,0:T(8,128)S(1)}, u32[]{:S(2)}, u32[]{:S(2)}) async-start(f32[32,8,256]{2,1,0:T(8,128)} %get-tuple-element.11), calls=%async_computation | async-start | bytes 524288 | tf_op jit(solution)/shard_map/all_to_all | solution.py:325
  14.8 1.0 %collective-permute-start = (f32[1,8,128]{2,1,0:T(8,128)S(1)}, f32[1,8,128]{2,1,0:T(8,128)S(1)}, u32[]{:S(2)}, u32[]{:S(2)}) collective-permute-start(f32[1,8,128]{2,1,0:T(8,128)S(1)} %get-tuple-element.10), channel_id=1, source_target_pairs={{0,1},{1,0},{2,3},{3,2},{4,5},{5,4},{6,7},{7,6},{8,9},{9,8},{10,11... | collective-permute-start | bytes 12296 | tf_op jit(solution)/shard_map/ppermute | solution.py:326
  15.9 0.8 %collective-permute-done = f32[1,8,128]{2,1,0:T(8,128)S(1)} collective-permute-done((f32[1,8,128]{2,1,0:T(8,128)S(1)}, f32[1,8,128]{2,1,0:T(8,128)S(1)}, u32[]{:S(2)}, u32[]{:S(2)}) %collective-permute-start) | collective-permute-done | bytes 4128 | tf_op jit(solution)/shard_map/ppermute | solution.py:326
  16.7 1.2 %collective-permute-start.1 = (f32[2,8,128]{2,1,0:T(8,128)S(1)}, f32[2,8,128]{2,1,0:T(8,128)S(1)}, u32[]{:S(2)}, u32[]{:S(2)}) collective-permute-start(f32[2,8,128]{2,1,0:T(8,128)S(1)} %pad_maximum_fusion), channel_id=1, source_target_pairs={{0,64},{64,0},{128,192},{192,128},{1,65},{65,1},{129,193},{193,129... | collective-permute-start | bytes 24584 | tf_op jit(solution)/shard_map/ppermute | solution.py:327
  17.9 1.3 %collective-permute-done.1 = f32[2,8,128]{2,1,0:T(8,128)S(1)} collective-permute-done((f32[2,8,128]{2,1,0:T(8,128)S(1)}, f32[2,8,128]{2,1,0:T(8,128)S(1)}, u32[]{:S(2)}, u32[]{:S(2)}) %collective-permute-start.1) | collective-permute-done | bytes 8224 | tf_op jit(solution)/shard_map/ppermute | solution.py:327
  19.2 2.5 %collective-permute-start.2 = (f32[4,8,128]{2,1,0:T(8,128)S(1)}, f32[4,8,128]{2,1,0:T(8,128)S(1)}, u32[]{:S(2)}, u32[]{:S(2)}) collective-permute-start(f32[4,8,128]{2,1,0:T(8,128)S(1)} %constant_dynamic-update-slice_fusion.near_ref), channel_id=1, source_target_pairs={{0,192},{192,0},{64,128},{128,64},{1,193},{193,1},{65,129},{129,65... | collective-permute-start | bytes 49160 | tf_op jit(solution)/shard_map/ppermute | solution.py:328
  21.7 1.6 %collective-permute-done.2.far_ref = f32[4,8,128]{2,1,0:T(8,128)S(1)} collective-permute-done((f32[4,8,128]{2,1,0:T(8,128)S(1)}, f32[4,8,128]{2,1,0:T(8,128)S(1)}, u32[]{:S(2)}, u32[]{:S(2)}) %collective-permute-start.2) | collective-permute-done | bytes 16416 | tf_op jit(solution)/shard_map/ppermute | solution.py:328
  23.3 1.2 %all-to-all-done.src_ref = f32[32,8,256]{2,1,0:T(8,128)S(1)} async-done(((f32[32,8,256]{2,1,0:T(8,128)}), f32[32,8,256]{2,1,0:T(8,128)S(1)}, u32[]{:S(2)}, u32[]{:S(2)}) %all-to-all-start) | async-done | bytes 262176 | tf_op jit(solution)/shard_map/all_to_all | solution.py:325
  24.5 13.5 %pair_sums.1 = f32[8,8,128]{2,1,0:T(8,128)S(1)} custom-call(f32[4,8,128]{2,1,0:T(8,128)S(1)} %constant_dynamic-update-slice_fusion.near_ref, f32[4,8,128]{2,1,0:T(8,128)S(1)} %collective-permute-done.2.far_ref, f32[32,8,256]{2,1,0:T(8,128)S(1)} %all-to-all-done.src_ref), custom_call_target="tpu_custom_call" | custom-call | flops 400000000 | bytes 400000 | tf_op jit(solution)/shard_map/pair_sums/pallas_call | solution.py:236
  38.0 12.9 %all_to_all.10.part_ref = f32[8,8,128]{2,1,0:T(8,128)S(1)} all-to-all(f32[8,8,128]{2,1,0:T(8,128)S(1)} %pair_sums.1), channel_id=1, replica_groups=mesh['x'=4,'y'=4,'z'=8,'c'=2] {'x','c'}, dimensions={0} | all-to-all | bytes 65536 | tf_op jit(solution)/shard_map/all_to_all | solution.py:330
  51.0 0.6 %correct.1 = (f32[6,128]{1,0:T(8,128)}, f32[6,128]{1,0:T(8,128)}, f32[1,128]{1,0:T(1,128)}) custom-call(f32[16,128]{1,0:T(8,128)S(1)} %get-tuple-element.9.own_ref, f32[8,8,128]{2,1,0:T(8,128)S(1)} %all_to_all.10.part_ref), custom_call_target="tpu_custom_call" | custom-call | tf_op jit(solution)/shard_map/correct/pallas_call | solution.py:331
  (4 shorter events, 0.0 us)
Async XLA Ops:
  2.8 21.7 %all-to-all-start = ((f32[32,8,256]{2,1,0:T(8,128)}), f32[32,8,256]{2,1,0:T(8,128)S(1)}, u32[]{:S(2)}, u32[]{:S(2)}) async-start(f32[32,8,256]{2,1,0:T(8,128)} %get-tuple-element.11), calls=%async_computation | async-start | bytes 524288 | tf_op jit(solution)/shard_map/all_to_all | solution.py:325
  14.8 1.9 %collective-permute-start = (f32[1,8,128]{2,1,0:T(8,128)S(1)}, f32[1,8,128]{2,1,0:T(8,128)S(1)}, u32[]{:S(2)}, u32[]{:S(2)}) collective-permute-start(f32[1,8,128]{2,1,0:T(8,128)S(1)} %get-tuple-element.10), channel_id=1, source_target_pairs={{0,1},{1,0},{2,3},{3,2},{4,5},{5,4},{6,7},{7,6},{8,9},{9,8},{10,11... | collective-permute-start | bytes 12296 | tf_op jit(solution)/shard_map/ppermute | solution.py:326
  16.7 2.5 %collective-permute-start.1 = (f32[2,8,128]{2,1,0:T(8,128)S(1)}, f32[2,8,128]{2,1,0:T(8,128)S(1)}, u32[]{:S(2)}, u32[]{:S(2)}) collective-permute-start(f32[2,8,128]{2,1,0:T(8,128)S(1)} %pad_maximum_fusion), channel_id=1, source_target_pairs={{0,64},{64,0},{128,192},{192,128},{1,65},{65,1},{129,193},{193,129... | collective-permute-start | bytes 24584 | tf_op jit(solution)/shard_map/ppermute | solution.py:327
  19.2 4.1 %collective-permute-start.2 = (f32[4,8,128]{2,1,0:T(8,128)S(1)}, f32[4,8,128]{2,1,0:T(8,128)S(1)}, u32[]{:S(2)}, u32[]{:S(2)}) collective-permute-start(f32[4,8,128]{2,1,0:T(8,128)S(1)} %constant_dynamic-update-slice_fusion.near_ref), channel_id=1, source_target_pairs={{0,192},{192,0},{64,128},{128,64},{1,193},{193,1},{65,129},{129,65... | collective-permute-start | bytes 49160 | tf_op jit(solution)/shard_map/ppermute | solution.py:328
